TPU v7x, 32 devices: a whole 2x2x4 slice. The times are simulated.
32 devices in a mesh: groups: 2 (over x), row: 16 (over z, y, core).
Axes of the slice: x: 2, y: 2, z: 4, core: 2. Of those that a mesh axis runs over, the one named last changes fastest.
Arguments:
- matrix: float32 [32768, 1024], P(('groups', 'row')), parts along dimension 0, may hold values from -6 to 6
- leaf_vectors: float32 [4, 10240, 256], P('groups', 'row'), parts along dimension 0, may hold values from -0.25 to 0.25
- leaf_factors: float32 [4, 4096, 256], P('groups', 'row'), parts along dimension 0, as said below
- tree_vectors: float32 [4, 4096, 256], P('groups', 'row'), parts along dimension 0, may hold values from -0.375 to 0.375
- tree_factors: float32 [4, 4096, 256], P('groups', 'row'), parts along dimension 0, as said below
- leaf_blocks: int32 [4, 80], P('groups', 'row'), parts along dimension 0, may hold values from 0 to 7, as said below
- owner: int32 [4], P('groups'), parts along dimension 0, may hold values from 0 to 15
Outputs:
- updated: float32 [32768, 1024], P(('groups', 'row')), parts along dimension 0
There are 2 independent parts, one for each index of `groups`. A program takes and returns all parts, laid end to end along the dimension named above; each array names one. Nothing has to cross between parts.
Inputs may be any that keep to these rules, and one draw needn't show every extreme that they name: `leaf_blocks`: in step s, the 5 entries of each grid block are distinct row-block numbers of that block: first the 2 blocks of the step's panel rows in order, last the block's final row block, the others between them. `leaf_factors`: each 256 x 256 factor is upper triangular. `tree_factors`: each 256 x 256 factor is upper triangular.
All inputs are finite; a program needn't handle non-finite values.
Results may differ from a plain program's by a relative error of at most 0.0001.
Values sent between devices are 32-bit elements; how exact they have to be, the bound alone decides.
A program may use at most 128 MiB of HBM per device.

v0:
```python
import functools

import jax
import jax.numpy as jnp
from jax import lax
from jax.experimental import pallas as pl
from jax.experimental.pallas import tpu as pltpu
from jax.sharding import PartitionSpec as P

BLK = 128
STEPS = 2
COLS_PER_LEAF = 256

NN = (((1,), (0,)), ((), ()))
TN = (((0,), (0,)), ((), ()))
NT = (((1,), (1,)), ((), ()))


def split(value):
    high = value.astype(jnp.bfloat16)
    low = (value - high.astype(jnp.float32)).astype(jnp.bfloat16)
    return high, low


def product3(left, right, dims):
    def one(a, b):
        return lax.dot_general(a, b, dims, preferred_element_type=jnp.float32)

    return one(left[0], right[0]) + (one(left[0], right[1]) + one(left[1], right[0]))


def leaf_kernel(listed, m_ref, y_ref, l_ref, out_ref, tops_ref, yh, yl, yth, ytl, lth, ltl):
    panel = l_ref.shape[1]
    listed_count = y_ref.shape[1] // BLK

    @pl.when(pl.program_id(0) == 0)
    def _():
        for s in range(STEPS):
            high, low = split(y_ref[s])
            yh[s], yl[s] = high, low
            high, low = split(y_ref[s].T)
            yth[s], ytl[s] = high, low
            high, low = split(l_ref[s].T)
            lth[s], ltl[s] = high, low

    out_ref[...] = m_ref[...]
    for s in range(STEPS):
        starts = [pl.multiple_of(listed[s, k] * BLK, BLK) for k in range(listed_count)]
        gathered = jnp.concatenate([out_ref[pl.ds(start, BLK), :] for start in starts], axis=0)
        projected = product3((yth[s], ytl[s]), split(gathered), NN)
        update = product3((lth[s], ltl[s]), split(projected), NN)
        renewed = gathered - product3((yh[s], yl[s]), split(update), NN)
        for k, start in enumerate(starts):
            out_ref[pl.ds(start, BLK), :] = renewed[k * BLK : (k + 1) * BLK]
    for s in range(STEPS):
        tops_ref[:, s * panel : (s + 1) * panel] = out_ref[s * panel : (s + 1) * panel, :].T


def leaf(matrix, leaf_vectors, leaf_factors, leaf_blocks):
    rows, columns = matrix.shape
    width = COLS_PER_LEAF
    steps, leaf_rows, panel = leaf_vectors.shape
    return pl.pallas_call(
        leaf_kernel,
        out_shape=(
            jax.ShapeDtypeStruct((rows, columns), jnp.float32),
            jax.ShapeDtypeStruct((columns, steps * panel), jnp.float32),
        ),
        grid_spec=pltpu.PrefetchScalarGridSpec(
            num_scalar_prefetch=1,
            grid=(columns // width,),
            in_specs=[
                pl.BlockSpec((rows, width), lambda c, *_: (0, c)),
                pl.BlockSpec(leaf_vectors.shape, lambda c, *_: (0, 0, 0)),
                pl.BlockSpec(leaf_factors.shape, lambda c, *_: (0, 0, 0)),
            ],
            out_specs=[
                pl.BlockSpec((rows, width), lambda c, *_: (0, c)),
                pl.BlockSpec((width, steps * panel), lambda c, *_: (c, 0)),
            ],
            scratch_shapes=[
                pltpu.VMEM((steps, leaf_rows, panel), jnp.bfloat16),
                pltpu.VMEM((steps, leaf_rows, panel), jnp.bfloat16),
                pltpu.VMEM((steps, panel, leaf_rows), jnp.bfloat16),
                pltpu.VMEM((steps, panel, leaf_rows), jnp.bfloat16),
                pltpu.VMEM((steps, panel, panel), jnp.bfloat16),
                pltpu.VMEM((steps, panel, panel), jnp.bfloat16),
            ],
        ),
    )(leaf_blocks, matrix, leaf_vectors, leaf_factors)


def tree_kernel(upper, lower, x_ref, u_ref, f_ref, out_ref):
    node, step = pl.program_id(0), pl.program_id(1)
    panel = u_ref.shape[2]
    half = panel // 2

    @pl.when((node == 0) & (step == 0))
    def _():
        out_ref[...] = x_ref[...]

    u = split(u_ref[0, 0])
    packed = f_ref[0, 0]
    bottom = jnp.concatenate([jnp.zeros((half, half), jnp.float32), packed[:, panel:]], axis=1)
    f = split(jnp.concatenate([packed[:, :panel], bottom], axis=0))
    for s in range(STEPS):

        @pl.when(step == s)
        def _():
            place = pl.ds(s * panel, panel)
            a, b = upper[s, node], lower[s, node]
            xa, xb = out_ref[a, :, place], out_ref[b, :, place]
            total = xa + product3(split(xb), u, NN)
            w = product3(split(total), f, NN)
            out_ref[a, :, place] = xa - w
            out_ref[b, :, place] = xb - product3(split(w), u, NT)


def tree(gathered, vectors, factors, upper, lower):
    devices, steps, panel, _ = vectors.shape
    return pl.pallas_call(
        tree_kernel,
        out_shape=jax.ShapeDtypeStruct(gathered.shape, jnp.float32),
        grid_spec=pltpu.PrefetchScalarGridSpec(
            num_scalar_prefetch=2,
            grid=(devices - 1, steps),
            in_specs=[
                pl.BlockSpec(gathered.shape, lambda n, s, *_: (0, 0, 0)),
                pl.BlockSpec((1, 1, panel, panel), lambda n, s, up, lo: (lo[s, n], s, 0, 0)),
                pl.BlockSpec((1, 1) + factors.shape[2:], lambda n, s, up, lo: (lo[s, n], s, 0, 0)),
            ],
            out_specs=pl.BlockSpec(gathered.shape, lambda n, s, *_: (0, 0, 0)),
        ),
    )(upper, lower, gathered, vectors, factors)


def place_kernel(t_ref, _, out_ref):
    out_ref[...] = t_ref[...].T


def place(tops, work):
    columns, rows = tops.shape
    width = 256
    return pl.pallas_call(
        place_kernel,
        out_shape=jax.ShapeDtypeStruct(work.shape, jnp.float32),
        grid=(columns // width,),
        in_specs=[
            pl.BlockSpec((width, rows), lambda c: (c, 0)),
            pl.BlockSpec(memory_space=pl.ANY),
        ],
        out_specs=pl.BlockSpec((rows, width), lambda c: (0, c)),
        input_output_aliases={1: 0},
    )(tops, work)


def pairs(row_count):
    uppers, lowers = [], []
    gap = 1
    while gap < row_count:
        for start in range(0, row_count, 2 * gap):
            uppers.append(start)
            lowers.append(start + gap)
        gap *= 2
    return jnp.array(uppers, jnp.int32), jnp.array(lowers, jnp.int32)


def shards(matrix, leaf_vectors, leaf_factors, tree_vectors, tree_factors, leaf_blocks, owner):
    row_count = lax.axis_size("row")
    columns = matrix.shape[1]
    panel = tree_vectors.shape[2]
    half = panel // 2
    packed = jnp.concatenate([tree_factors[:, :half], tree_factors[:, half:, half:]], axis=2)
    vectors = lax.all_gather(tree_vectors, "row")
    factors = lax.all_gather(packed, "row")
    work, tops = leaf(matrix, leaf_vectors, leaf_factors, leaf_blocks)
    spread = tops.reshape(row_count, columns // row_count, STEPS * panel)
    gathered = lax.all_to_all(spread, "row", 0, 0)
    uppers, lowers = pairs(row_count)
    upper = (uppers[None] + owner[:, None]) % row_count
    lower = (lowers[None] + owner[:, None]) % row_count
    done = tree(gathered, vectors, factors, upper, lower)
    back = lax.all_to_all(done, "row", 0, 0)
    return place(back.reshape(columns, STEPS * panel), work)


def solution(mesh):
    return jax.shard_map(
        shards,
        mesh=mesh,
        in_specs=(
            P(("groups", "row"), None),
            P("groups", "row", None),
            P("groups", "row", None),
            P("groups", "row", None),
            P("groups", "row", None),
            P("groups", "row"),
            P("groups"),
        ),
        out_specs=P(("groups", "row"), None),
        check_vma=False,
    )
```

profile of v0, /device:TPU:11, one launch (start us, length us, event | category | flops | bytes accessed | tf_op | source)
XLA Modules:
  0.0 273.8 jit_solution(2989278103987318698)
XLA Ops:
  6.5 0.0 all-gather.7.cloned.1.call-start
  6.5 1.0 slice.6
  7.5 0.9 slice.7
  8.4 0.8 pad_maximum_fusion
  9.2 0.0 all-gather.7.cloned.1.call-update
  9.2 0.0 all-gather.5.cloned.1.call-start
  9.3 0.7 all-gather.5.cloned.1.call-update
  10.0 0.0 copy-start.1
  10.0 0.0 copy-start.2
  10.0 0.0 copy-start.3
  10.0 18.8 %shard_map.91 = (f32[1024,1024]{1,0:T(8,128)}, f32[1024,512]{1,0:T(8,128)}) custom-call(s32[2,5]{1,0:T(2,128)} %listed.1, f32[1024,1024]{1,0:T(8,128)} %m_ref.1, f32[2,640,256]{2,1,0:T(8,128)} %y_ref.1, f32[2,256,256]{2,1,0:T(8,128)} %l_ref.1), custom_call_target="tpu_custom_call" | custom-call | tf_op jit(solution)/shard_map/pallas_call | solution.py:63
  28.8 6.6 %all-to-all-start = ((f32[16,64,512]{2,1,0:T(8,128)}), f32[16,64,512]{2,1,0:T(8,128)S(1)}, u32[]{:S(2)}, u32[]{:S(2)}) async-start(f32[16,64,512]{2,1,0:T(8,128)} %bitcast.7), calls=%async_computation | async-start | bytes 4194304 | tf_op jit(solution)/shard_map/all_to_all | solution.py:178
  35.4 0.0 copy-done.1
  35.4 0.0 copy-done.2
  35.4 0.0 copy-done.3
  35.4 0.6 and_select_fusion
  36.1 70.6 %all-to-all-done.x_ref = f32[16,64,512]{2,1,0:T(8,128)S(1)} async-done(((f32[16,64,512]{2,1,0:T(8,128)}), f32[16,64,512]{2,1,0:T(8,128)S(1)}, u32[]{:S(2)}, u32[]{:S(2)}) %all-to-all-start) | async-done | bytes 2097184 | tf_op jit(solution)/shard_map/all_to_all | solution.py:178
  106.7 0.0 copy-start
  106.7 0.0 all-gather.7.cloned.1.call-done
  106.7 73.4 %all-gather.5.cloned.1.call-done = f32[32,256,256]{2,1,0:T(8,128)} async-done(((f32[2,256,256]{2,1,0:T(8,128)}), f32[32,256,256]{2,1,0:T(8,128)}) %all-gather.5.cloned.1.call-update) | async-done | bytes 8388624 | tf_op jit(solution)/shard_map/all_gather | solution.py:174
  180.1 0.0 copy-done
  180.1 29.9 %shard_map.92 = f32[16,64,512]{2,1,0:T(8,128)} custom-call(s32[2,15]{1,0:T(2,128)} %get-tuple-element.10.upper, s32[2,15]{1,0:T(2,128)} %get-tuple-element.9.lower, f32[16,64,512]{2,1,0:T(8,128)} %copy-done, f32[16,2,256,256]{3,2,1,0:T(8,128)} %bitcast.4, f32[16,2,128,384]{3,2,1,0:T(8,128)} %bitcast.6), custom_call_target="tpu_custom_call" | custom-call | tf_op jit(solution)/shard_map/pallas_call | solution.py:121
  210.0 52.8 %all_to_all.10 = f32[16,64,512]{2,1,0:T(8,128)} all-to-all(f32[16,64,512]{2,1,0:T(8,128)} %shard_map.92), channel_id=1, replica_groups=mesh['groups'=2,'row'=16] {'row'}, dimensions={0} | all-to-all | bytes 4194304 | tf_op jit(solution)/shard_map/all_to_all | solution.py:183
  262.8 4.1 %shard_map.93 = f32[1024,1024]{1,0:T(8,128)} custom-call(f32[1024,512]{1,0:T(8,128)} %bitcast.5, f32[1024,1024]{1,0:T(8,128)} %get-tuple-element.8._), custom_call_target="tpu_custom_call", output_to_operand_aliasing={{}: (1, {})} | custom-call | tf_op jit(solution)/shard_map/pallas_call | solution.py:144
Async XLA Ops:
  6.5 100.2 %all-gather.7.cloned.1.call-start = ((), (), s32[]{:S(2)}) async-start(), calls=%async_computation.3 | async-start | bytes 6684672 | tf_op jit(solution)/shard_map/all_gather | solution.py:175
  9.2 170.9 %all-gather.5.cloned.1.call-start = ((), (), s32[]{:S(2)}) async-start(), calls=%async_computation.2 | async-start | bytes 8912896 | tf_op jit(solution)/shard_map/all_gather | solution.py:174
  10.0 25.4 %copy-start.1 = (s32[2]{0:T(128)S(1)}, s32[2]{0:T(128)}, u32[]{:S(2)}) copy-start(s32[2]{0:T(128)} %param.15) | copy-start | bytes 28
  10.0 25.4 %copy-start.2 = (s32[15]{0:T(128)S(1)}, s32[15]{0:T(128)}, u32[]{:S(2)}) copy-start(s32[15]{0:T(128)} %constant.24.clone) | copy-start | bytes 184
  10.0 25.4 %copy-start.3 = (s32[15]{0:T(128)S(1)}, s32[15]{0:T(128)}, u32[]{:S(2)}) copy-start(s32[15]{0:T(128)} %constant.25.clone) | copy-start | bytes 184
  28.8 77.9 %all-to-all-start = ((f32[16,64,512]{2,1,0:T(8,128)}), f32[16,64,512]{2,1,0:T(8,128)S(1)}, u32[]{:S(2)}, u32[]{:S(2)}) async-start(f32[16,64,512]{2,1,0:T(8,128)} %bitcast.7), calls=%async_computation | async-start | bytes 4194304 | tf_op jit(solution)/shard_map/all_to_all | solution.py:178
  106.7 73.4 %copy-start = (f32[16,64,512]{2,1,0:T(8,128)}, f32[16,64,512]{2,1,0:T(8,128)S(1)}, u32[]{:S(2)}) copy-start(f32[16,64,512]{2,1,0:T(8,128)S(1)} %all-to-all-done.x_ref) | copy-start | bytes 6291460
Sparse Core Ops, SparseCore 0:
  9.6 91.3 all-gather.6
  103.2 76.8 all-gather.4
where the time goes:
time: 275 us; the launch traced here: 274 us
  waiting for transfers between devices  145 us (53%)
  Pallas kernels  52.8 us (19%)
  blocking collectives  52.8 us (19%)
  between operations  13.5 us (5%)
  starting transfers between devices  6.62 us (2%)
    all_gather x1, waiting for transfers between devices, shards(): vectors = lax.all_gather(tree_vectors, 'row')  73.4 us
    all_to_all x1, waiting for transfers between devices, shards(): gathered = lax.all_to_all(spread, 'row', 0, 0)  70.6 us
    all_to_all x1, blocking collectives, shards(): back = lax.all_to_all(done, 'row', 0, 0)  52.8 us
    pallas_call x1, Pallas kernels, tree(): pl.pallas_call(tree_kernel, out_shape=jax.ShapeDtypeStruct(gathered.shape...  29.9 us
    pallas_call x1, Pallas kernels, leaf(): pl.pallas_call(leaf_kernel, out_shape=(jax.ShapeDtypeStruct((rows, column...  18.8 us
    all_to_all x1, starting transfers between devices, shards(): gathered = lax.all_to_all(spread, 'row', 0, 0)  6.58 us
  transfers between devices with their start and end apart: 3, of which 2 were waited for; matrix products, arithmetic and copies ran while one was open for 0% of the time, Pallas kernels for 7%

commit v1 on v0

v1 whole, which is shorter than its diff:
```python
import functools

import jax
import jax.numpy as jnp
from jax import lax
from jax.experimental import pallas as pl
from jax.experimental.pallas import tpu as pltpu
from jax.sharding import PartitionSpec as P

BLK = 128
STEPS = 2
COLS_PER_LEAF = 256

NN = (((1,), (0,)), ((), ()))
TN = (((0,), (0,)), ((), ()))
NT = (((1,), (1,)), ((), ()))


def split(value):
    high = value.astype(jnp.bfloat16)
    low = (value - high.astype(jnp.float32)).astype(jnp.bfloat16)
    return high, low


def product3(left, right, dims):
    def one(a, b):
        return lax.dot_general(a, b, dims, preferred_element_type=jnp.float32)

    return one(left[0], right[0]) + (one(left[0], right[1]) + one(left[1], right[0]))


def leaf_kernel(listed, odd, m_ref, y_ref, l_ref, u_ref, out_ref, *rest):
    tops_refs, (yh, yl, yth, ytl, lth, ltl) = rest[:STEPS], rest[STEPS:]
    panel = l_ref.shape[1]
    listed_count = y_ref.shape[1] // BLK

    @pl.when(pl.program_id(0) == 0)
    def _():
        for s in range(STEPS):
            high, low = split(y_ref[s])
            yh[s], yl[s] = high, low
            high, low = split(y_ref[s].T)
            yth[s], ytl[s] = high, low
            high, low = split(l_ref[s].T)
            lth[s], ltl[s] = high, low

    out_ref[...] = m_ref[...]
    for s in range(STEPS):
        starts = [pl.multiple_of(listed[s, k] * BLK, BLK) for k in range(listed_count)]
        gathered = jnp.concatenate([out_ref[pl.ds(start, BLK), :] for start in starts], axis=0)
        projected = product3((yth[s], ytl[s]), split(gathered), NN)
        update = product3((lth[s], ltl[s]), split(projected), NN)
        renewed = gathered - product3((yh[s], yl[s]), split(update), NN)
        for k, start in enumerate(starts):
            out_ref[pl.ds(start, BLK), :] = renewed[k * BLK : (k + 1) * BLK]
    for s in range(STEPS):
        turned = out_ref[s * panel : (s + 1) * panel, :].T
        tops_refs[s][...] = turned

        @pl.when(odd[s] == 1)
        def _():
            tops_refs[s][...] = product3(split(turned), split(u_ref[s]), NN)


def leaf(matrix, leaf_vectors, leaf_factors, tree_vectors, leaf_blocks, odd):
    rows, columns = matrix.shape
    width = COLS_PER_LEAF
    steps, leaf_rows, panel = leaf_vectors.shape
    return pl.pallas_call(
        leaf_kernel,
        out_shape=(
            jax.ShapeDtypeStruct((rows, columns), jnp.float32),
            *[jax.ShapeDtypeStruct((columns, panel), jnp.float32)] * steps,
        ),
        grid_spec=pltpu.PrefetchScalarGridSpec(
            num_scalar_prefetch=2,
            grid=(columns // width,),
            in_specs=[
                pl.BlockSpec((rows, width), lambda c, *_: (0, c)),
                pl.BlockSpec(leaf_vectors.shape, lambda c, *_: (0, 0, 0)),
                pl.BlockSpec(leaf_factors.shape, lambda c, *_: (0, 0, 0)),
                pl.BlockSpec(tree_vectors.shape, lambda c, *_: (0, 0, 0)),
            ],
            out_specs=[
                pl.BlockSpec((rows, width), lambda c, *_: (0, c)),
                *[pl.BlockSpec((width, panel), lambda c, *_: (c, 0))] * steps,
            ],
            scratch_shapes=[
                pltpu.VMEM((steps, leaf_rows, panel), jnp.bfloat16),
                pltpu.VMEM((steps, leaf_rows, panel), jnp.bfloat16),
                pltpu.VMEM((steps, panel, leaf_rows), jnp.bfloat16),
                pltpu.VMEM((steps, panel, leaf_rows), jnp.bfloat16),
                pltpu.VMEM((steps, panel, panel), jnp.bfloat16),
                pltpu.VMEM((steps, panel, panel), jnp.bfloat16),
            ],
        ),
    )(leaf_blocks, odd, matrix, leaf_vectors, leaf_factors, tree_vectors)


def corner_masks(half):
    row = lax.broadcasted_iota(jnp.int32, (half, half), 0)
    column = lax.broadcasted_iota(jnp.int32, (half, half), 1)
    return row < column, row == column


def pack_kernel(odd, own_ref, other_ref, f_ref, *out_refs):
    half = own_ref.shape[1]
    above, on = corner_masks(half)
    for s, out_ref in enumerate(out_refs):
        out_ref[:half, :] = own_ref[s]

        @pl.when(odd[s] == 1)
        def _():
            out_ref[:half, :] = other_ref[s]

        first = f_ref[s, :half, :half]
        second = f_ref[s, half:, half:]
        out_ref[half : 2 * half, :half] = jnp.where(above | on, first, second.T)
        out_ref[half : 2 * half, half:] = f_ref[s, :half, half:]
        diagonal = jnp.sum(jnp.where(on, second, 0.0), axis=0, keepdims=True)
        line = jnp.concatenate([diagonal, jnp.zeros_like(diagonal)], axis=1)
        out_ref[2 * half :, :] = jnp.broadcast_to(line, (8, 2 * half))


def pack(own, other, factors, odd):
    steps, half, panel = own.shape
    shape = (panel + 8, panel)
    return pl.pallas_call(
        pack_kernel,
        out_shape=[jax.ShapeDtypeStruct(shape, jnp.float32)] * steps,
        grid_spec=pltpu.PrefetchScalarGridSpec(
            num_scalar_prefetch=1,
            grid=(1,),
            in_specs=[
                pl.BlockSpec(own.shape, lambda c, *_: (0, 0, 0)),
                pl.BlockSpec(other.shape, lambda c, *_: (0, 0, 0)),
                pl.BlockSpec(factors.shape, lambda c, *_: (0, 0, 0)),
            ],
            out_specs=[pl.BlockSpec(shape, lambda c, *_: (0, 0))] * steps,
        ),
    )(odd, own, other, factors)


def tree_kernel(upper, lower, x_ref, g_ref, out_ref):
    node = pl.program_id(0)
    panel = g_ref.shape[2]
    half = panel // 2
    first_level = x_ref.shape[0] // 2

    @pl.when(node == 0)
    def _():
        out_ref[...] = x_ref[...]

    a, b = upper[node], lower[node]
    slot = lax.rem(b, 2)
    above, on = corner_masks(half)
    corner = g_ref[slot, half : 2 * half, :half]
    diagonal = g_ref[slot, 2 * half : 2 * half + 1, :half]
    top = jnp.concatenate(
        [jnp.where(above | on, corner, 0.0), g_ref[slot, half : 2 * half, half:]], axis=1
    )
    last = jnp.where(above, corner.T, jnp.where(on, diagonal, 0.0))
    bottom = jnp.concatenate([jnp.zeros_like(last), last], axis=1)
    f = split(jnp.concatenate([top, bottom], axis=0))
    xa, xb = out_ref[a], out_ref[b]

    @pl.when(node < first_level)
    def _():
        w = product3(split(xa + xb), f, NN)
        out_ref[a] = xa - w
        out_ref[b] = w

    @pl.when(node >= first_level)
    def _():
        u = split(jnp.concatenate([g_ref[0, :half, :], g_ref[1, :half, :]], axis=0))
        w = product3(split(xa + product3(split(xb), u, NN)), f, NN)
        out_ref[a] = xa - w
        out_ref[b] = xb - product3(split(w), u, NT)


def tree(spread, reflectors, upper, lower):
    devices = spread.shape[0]
    return pl.pallas_call(
        tree_kernel,
        out_shape=jax.ShapeDtypeStruct(spread.shape, jnp.float32),
        grid_spec=pltpu.PrefetchScalarGridSpec(
            num_scalar_prefetch=2,
            grid=(devices - 1,),
            in_specs=[
                pl.BlockSpec(spread.shape, lambda n, *_: (0, 0, 0)),
                pl.BlockSpec((2,) + reflectors.shape[1:], lambda n, up, lo: (lo[n] // 2, 0, 0)),
            ],
            out_specs=pl.BlockSpec(spread.shape, lambda n, *_: (0, 0, 0)),
        ),
    )(upper, lower, spread, reflectors)


def place_kernel(odd, back_ref, u_ref, work_ref, out_ref):
    @pl.when(odd[0] == 0)
    def _():
        out_ref[...] = back_ref[...].T

    @pl.when(odd[0] == 1)
    def _():
        out_ref[...] = work_ref[...] - product3(split(u_ref[...]), split(back_ref[...]), NT)


def place(step, back, vectors, work, odd):
    columns, panel = back.shape
    width = COLS_PER_LEAF
    return pl.pallas_call(
        place_kernel,
        out_shape=jax.ShapeDtypeStruct(work.shape, jnp.float32),
        grid_spec=pltpu.PrefetchScalarGridSpec(
            num_scalar_prefetch=1,
            grid=(columns // width,),
            in_specs=[
                pl.BlockSpec((width, panel), lambda c, *_: (c, 0)),
                pl.BlockSpec((panel, panel), lambda c, *_: (0, 0)),
                pl.BlockSpec((panel, width), lambda c, *_: (step, c)),
            ],
            out_specs=pl.BlockSpec((panel, width), lambda c, *_: (step, c)),
        ),
        input_output_aliases={3: 0},
    )(odd, back, vectors, work)


def pairs(row_count):
    uppers, lowers = [], []
    gap = 1
    while gap < row_count:
        for start in range(0, row_count, 2 * gap):
            uppers.append(start)
            lowers.append(start + gap)
        gap *= 2
    return jnp.array(uppers, jnp.int32), jnp.array(lowers, jnp.int32)


def shards(matrix, leaf_vectors, leaf_factors, tree_vectors, tree_factors, leaf_blocks, owner):
    row_count = lax.axis_size("row")
    my_index = lax.axis_index("row")
    columns = matrix.shape[1]
    panel = tree_vectors.shape[2]
    half = panel // 2
    core = my_index % 2
    odd = ((my_index - owner) % 2).astype(jnp.int32)
    own = lax.dynamic_slice_in_dim(tree_vectors, core * half, half, axis=1)
    asked = lax.dynamic_slice_in_dim(tree_vectors, (1 - core) * half, half, axis=1)
    other = lax.ppermute(asked, "row", [(i, i ^ 1) for i in range(row_count)])
    packed = pack(own, other, tree_factors, odd)
    reflectors = [lax.all_gather(p, "row") for p in packed]
    work, *tops = leaf(matrix, leaf_vectors, leaf_factors, tree_vectors, leaf_blocks, odd)
    uppers, lowers = pairs(row_count)
    for s in range(STEPS):
        spread = tops[s].reshape(row_count, columns // row_count, panel)
        spread = lax.all_to_all(spread, "row", 0, 0)
        upper, lower = (uppers + owner[s]) % row_count, (lowers + owner[s]) % row_count
        done = tree(spread, reflectors[s], upper, lower)
        back = lax.all_to_all(done, "row", 0, 0).reshape(columns, panel)
        work = place(s, back, tree_vectors[s], work, odd[s : s + 1])
    return work


def solution(mesh):
    return jax.shard_map(
        shards,
        mesh=mesh,
        in_specs=(
            P(("groups", "row"), None),
            P("groups", "row", None),
            P("groups", "row", None),
            P("groups", "row", None),
            P("groups", "row", None),
            P("groups", "row"),
            P("groups"),
        ),
        out_specs=P(("groups", "row"), None),
        check_vma=False,
    )
```

time: 275 us -> 221 us (0.80)
  waiting for transfers between devices: 145 us -> 68.8 us
  starting transfers between devices: 6.62 us -> 17.3 us
  Pallas kernels: 52.8 us -> 62.9 us
  blocking collectives: 52.8 us -> 48.9 us
  local copies, waits for them, and re-layouts: 1.92 us -> 5.57 us
    all_gather x2, waiting for transfers between devices: 73.4 us -> 33 us  [shards(): reflectors = [lax.all_gather(p, 'row') for p in packed]]
    all_to_all x1 -> x3, waiting for transfers between devices: 70.6 us -> 35.1 us  [the longest x2 18.9 us: shards(): back = lax.all_to_all(done, 'row', 0, 0).reshape(columns, panel)]
    all_to_all x1 -> x3, starting transfers between devices: 6.58 us -> 16.5 us  [the longest x2 11.6 us: shards(): back = lax.all_to_all(done, 'row', 0, 0).reshape(columns, panel)]
    pallas_call x1 -> x2, Pallas kernels: 4.11 us -> 9.41 us  [place(): pl.pallas_call(place_kernel, out_shape=jax.ShapeDtypeStruct(work.shape, j...]
    all_to_all x1, blocking collectives: 52.8 us -> 48.9 us  [shards(): spread = lax.all_to_all(spread, 'row', 0, 0)]
    pallas_call x1 -> x3, Pallas kernels: 29.9 us -> 32.9 us  [the longest x2 30.1 us: tree(): pl.pallas_call(tree_kernel, out_shape=jax.ShapeDtypeStruct(spread.shape,...]
  transfers between devices with their start and end apart: 3 -> 6, of which waited for: 2 -> 3; matrix products, arithmetic and copies ran while one was open for 0% -> 2% of each run, Pallas kernels for 7% -> 25%
where the time goes in v1:
time: 221 us; the launch traced here: 220 us
  waiting for transfers between devices  68.8 us (31%)
  Pallas kernels  62.9 us (28%)
  blocking collectives  48.9 us (22%)
  starting transfers between devices  17.3 us (8%)
  between operations  13.4 us (6%)
  local copies, waits for them, and re-layouts  5.57 us (3%)
  other arithmetic  3.04 us (1%)
    all_to_all x1, blocking collectives, shards(): spread = lax.all_to_all(spread, 'row', 0, 0)  48.9 us
    all_gather x2, waiting for transfers between devices, shards(): reflectors = [lax.all_gather(p, 'row') for p in packed]  33 us
    pallas_call x2, Pallas kernels, tree(): pl.pallas_call(tree_kernel, out_shape=jax.ShapeDtypeStruct(spread.shape,...  30.1 us
    pallas_call x1, Pallas kernels, leaf(): pl.pallas_call(leaf_kernel, out_shape=(jax.ShapeDtypeStruct((rows, column...  20.6 us
    all_to_all x2, waiting for transfers between devices, shards(): back = lax.all_to_all(done, 'row', 0, 0).reshape(columns, panel)  18.9 us
    all_to_all x1, waiting for transfers between devices, shards(): spread = lax.all_to_all(spread, 'row', 0, 0)  16.1 us
    all_to_all x2, starting transfers between devices, shards(): back = lax.all_to_all(done, 'row', 0, 0).reshape(columns, panel)  11.6 us
    pallas_call x2, Pallas kernels, place(): pl.pallas_call(place_kernel, out_shape=jax.ShapeDtypeStruct(work.shape, j...  9.41 us
  transfers between devices with their start and end apart: 6, of which 3 were waited for; matrix products, arithmetic and copies ran while one was open for 2% of the time, Pallas kernels for 25%

profile of v1, /device:TPU:11, one launch (start us, length us, event | category | flops | bytes accessed | tf_op | source)
XLA Modules:
  0.0 219.9 jit_solution(3537074638429027439)
XLA Ops:
  6.5 0.0 all-gather.7.cloned.1.call-start
  6.5 1.8 constant_dynamic-slice_fusion
  8.3 0.7 collective-permute-start
  9.0 1.2 and_select_fusion.4.odd
  10.2 0.0 collective-permute-done.other_ref
  10.2 0.7 copy-done.4
  10.9 2.8 %shard_map.92 = (f32[264,256]{1,0:T(8,128)}, f32[264,256]{1,0:T(8,128)}) custom-call(s32[2]{0:T(128)} %and_select_fusion.4.odd, f32[2,128,256]{2,1,0:T(8,128)} %get-tuple-element.18.own_ref, f32[2,128,256]{2,1,0:T(8,128)} %copy-done.4, f32[2,256,256]{2,1,0:T(8,128)} %f_ref.1), custom_call_target="tpu_custom_call" | custom-call | tf_op jit(solution)/shard_map/pallas_call | solution.py:128
  13.7 0.0 all-gather.7.cloned.1.call-update
  13.7 0.0 all-gather.5.cloned.1.call-start
  13.8 0.7 all-gather.5.cloned.1.call-update
  14.5 0.0 copy-start.6
  14.5 0.0 copy-start.7
  14.5 0.0 copy-start.8
  14.5 20.6 %shard_map.91 = (f32[1024,1024]{1,0:T(8,128)}, f32[1024,256]{1,0:T(8,128)}, f32[1024,256]{1,0:T(8,128)}) custom-call(s32[2,5]{1,0:T(2,128)} %listed.1, s32[2]{0:T(128)} %and_select_fusion.4.odd, f32[1024,1024]{1,0:T(8,128)} %m_ref.1, f32[2,640,256]{2,1,0:T(8,128)} %y_ref.1, f32[2,256,256]{2,1,0:T(8,128)} %l_ref.1, f32[2,256,256]{2,1,0:T(8,128)} %u_ref.1), custom_call_target="tpu_custom_call" | custom-call | tf_op jit(solution)/shard_map/pallas_call | solution.py:69
  35.1 48.9 %all_to_all.20.x_ref = f32[16,64,256]{2,1,0:T(8,128)} all-to-all(f32[16,64,256]{2,1,0:T(8,128)} %bitcast.17), channel_id=1, replica_groups=mesh['groups'=2,'row'=16] {'row'}, dimensions={0} | all-to-all | bytes 2097152 | tf_op jit(solution)/shard_map/all_to_all | solution.py:256
  84.0 4.9 %all-to-all-start = ((f32[16,64,256]{2,1,0:T(8,128)}), f32[16,64,256]{2,1,0:T(8,128)S(1)}, u32[]{:S(2)}, u32[]{:S(2)}) async-start(f32[16,64,256]{2,1,0:T(8,128)} %bitcast.16), calls=%async_computation | async-start | bytes 2097152 | tf_op jit(solution)/shard_map/all_to_all | solution.py:256
  88.9 0.6 fusion.5
  89.5 0.0 copy-done.8
  89.5 1.8 and_select_fusion
  91.4 15.0 %shard_map.94 = f32[16,64,256]{2,1,0:T(8,128)} custom-call(s32[15]{0:T(128)} %get-tuple-element.28.upper, s32[15]{0:T(128)} %get-tuple-element.19.lower, f32[16,64,256]{2,1,0:T(8,128)} %all_to_all.20.x_ref, f32[16,264,256]{2,1,0:T(8,128)} %bitcast.13), custom_call_target="tpu_custom_call" | custom-call | tf_op jit(solution)/shard_map/pallas_call | solution.py:183
  106.4 16.1 %all-to-all-done.x_ref = f32[16,64,256]{2,1,0:T(8,128)S(1)} async-done(((f32[16,64,256]{2,1,0:T(8,128)}), f32[16,64,256]{2,1,0:T(8,128)S(1)}, u32[]{:S(2)}, u32[]{:S(2)}) %all-to-all-start) | async-done | bytes 1048608 | tf_op jit(solution)/shard_map/all_to_all | solution.py:256
  122.5 4.7 %all-to-all-start.3 = ((f32[16,64,256]{2,1,0:T(8,128)}), f32[16,64,256]{2,1,0:T(8,128)S(1)}, u32[]{:S(2)}, u32[]{:S(2)}) async-start(f32[16,64,256]{2,1,0:T(8,128)} %shard_map.94), calls=%async_computation.3 | async-start | bytes 2097152 | tf_op jit(solution)/shard_map/all_to_all | solution.py:259
  127.2 33.0 %all-gather.5.cloned.1.call-done = f32[4224,256]{1,0:T(8,128)} async-done(((f32[264,256]{1,0:T(8,128)}), f32[4224,256]{1,0:T(8,128)}) %all-gather.5.cloned.1.call-update) | async-done | bytes 4325392 | tf_op jit(solution)/shard_map/all_gather | solution.py:251
  160.3 15.1 %shard_map.93 = f32[16,64,256]{2,1,0:T(8,128)} custom-call(s32[15]{0:T(128)} %get-tuple-element.27.upper, s32[15]{0:T(128)} %get-tuple-element.20.lower, f32[16,64,256]{2,1,0:T(8,128)} %copy-done.3, f32[16,264,256]{2,1,0:T(8,128)} %bitcast.12), custom_call_target="tpu_custom_call" | custom-call | tf_op jit(solution)/shard_map/pallas_call | solution.py:183
  175.4 0.0 all-to-all-done.3
  175.4 6.9 %all-to-all-start.1 = ((f32[16,64,256]{2,1,0:T(8,128)}), f32[16,64,256]{2,1,0:T(8,128)S(1)}, u32[]{:S(2)}, u32[]{:S(2)}) async-start(f32[16,64,256]{2,1,0:T(8,128)} %shard_map.93), calls=%async_computation.1 | async-start | bytes 2097152 | tf_op jit(solution)/shard_map/all_to_all | solution.py:259
  182.3 0.6 fusion.6
  182.9 0.8 slice_bitcast_fusion
  183.7 4.6 %shard_map.95.work_ref = f32[1024,1024]{1,0:T(8,128)} custom-call(s32[1]{0:T(128)} %get-tuple-element.25.odd, f32[1024,256]{1,0:T(8,128)} %bitcast.14, f32[256,256]{1,0:T(8,128)} %get-tuple-element.15.u_ref, f32[1024,1024]{1,0:T(8,128)} %get-tuple-element.14.work_ref), custom_call_target="tpu_custom_call", output_to_operand_aliasing={{}: (3, {})} | custom-call | tf_op jit(solution)/shard_map/pallas_call | solution.py:211
  188.3 18.9 %all-to-all-done.1 = f32[16,64,256]{2,1,0:T(8,128)S(1)} async-done(((f32[16,64,256]{2,1,0:T(8,128)}), f32[16,64,256]{2,1,0:T(8,128)S(1)}, u32[]{:S(2)}, u32[]{:S(2)}) %all-to-all-start.1) | async-done | bytes 1048608 | tf_op jit(solution)/shard_map/all_to_all | solution.py:259
  207.2 1.0 copy-done.2
  208.2 4.9 %shard_map.96 = f32[1024,1024]{1,0:T(8,128)} custom-call(s32[1]{0:T(128)} %get-tuple-element.26.odd, f32[1024,256]{1,0:T(8,128)} %bitcast.15, f32[256,256]{1,0:T(8,128)} %get-tuple-element.16.u_ref, f32[1024,1024]{1,0:T(8,128)} %shard_map.95.work_ref), custom_call_target="tpu_custom_call", output_to_operand_aliasing={{}: (3, {})} | custom-call | tf_op jit(solution)/shard_map/pallas_call | solution.py:211
  (13 shorter events, 0.0 us)
Async XLA Ops:
  6.5 84.8 %all-gather.7.cloned.1.call-start = ((), (), s32[]{:S(2)}) async-start(), calls=%async_computation.5 | async-start | bytes 4595712 | tf_op jit(solution)/shard_map/all_gather | solution.py:251
  8.3 1.9 collective-permute-start
  10.2 0.7 copy-start.4
  13.7 146.5 %all-gather.5.cloned.1.call-start = ((), (), s32[]{:S(2)}) async-start(), calls=%async_computation.4 | async-start | bytes 4595712 | tf_op jit(solution)/shard_map/all_gather | solution.py:251
  14.5 74.4 %copy-start.6 = (s32[2]{0:T(128)S(1)}, s32[2]{0:T(128)}, u32[]{:S(2)}) copy-start(s32[2]{0:T(128)} %param.15) | copy-start | bytes 28
  14.5 75.0 %copy-start.7 = (s32[15]{0:T(128)S(1)}, s32[15]{0:T(128)}, u32[]{:S(2)}) copy-start(s32[15]{0:T(128)} %constant.64.clone) | copy-start | bytes 184
  14.5 75.0 %copy-start.8 = (s32[15]{0:T(128)S(1)}, s32[15]{0:T(128)}, u32[]{:S(2)}) copy-start(s32[15]{0:T(128)} %constant.65.clone) | copy-start | bytes 184
  84.0 38.5 %all-to-all-start = ((f32[16,64,256]{2,1,0:T(8,128)}), f32[16,64,256]{2,1,0:T(8,128)S(1)}, u32[]{:S(2)}, u32[]{:S(2)}) async-start(f32[16,64,256]{2,1,0:T(8,128)} %bitcast.16), calls=%async_computation | async-start | bytes 2097152 | tf_op jit(solution)/shard_map/all_to_all | solution.py:256
  122.5 37.7 %copy-start.3 = (f32[16,64,256]{2,1,0:T(8,128)}, f32[16,64,256]{2,1,0:T(8,128)S(1)}, u32[]{:S(2)}) copy-start(f32[16,64,256]{2,1,0:T(8,128)S(1)} %all-to-all-done.x_ref) | copy-start | bytes 3145732
  122.5 52.9 %all-to-all-start.3 = ((f32[16,64,256]{2,1,0:T(8,128)}), f32[16,64,256]{2,1,0:T(8,128)S(1)}, u32[]{:S(2)}, u32[]{:S(2)}) async-start(f32[16,64,256]{2,1,0:T(8,128)} %shard_map.94), calls=%async_computation.3 | async-start | bytes 2097152 | tf_op jit(solution)/shard_map/all_to_all | solution.py:259
  160.3 22.1 %copy-start.5 = (s32[2]{0:T(128)S(1)}, s32[2]{0:T(128)}, u32[]{:S(2)}) copy-start(s32[2]{0:T(128)} %and_select_fusion.4.odd) | copy-start | bytes 28
  160.3 22.7 %copy-start = (f32[2,256,256]{2,1,0:T(8,128)S(1)}, f32[2,256,256]{2,1,0:T(8,128)}, u32[]{:S(2)}) copy-start(f32[2,256,256]{2,1,0:T(8,128)} %u_ref.1) | copy-start | bytes 1572868
  175.4 8.4 %copy-start.1 = (f32[16,64,256]{2,1,0:T(8,128)}, f32[16,64,256]{2,1,0:T(8,128)S(1)}, u32[]{:S(2)}) copy-start(f32[16,64,256]{2,1,0:T(8,128)S(1)} %all-to-all-done.3) | copy-start | bytes 3145732
  175.4 31.9 %all-to-all-start.1 = ((f32[16,64,256]{2,1,0:T(8,128)}), f32[16,64,256]{2,1,0:T(8,128)S(1)}, u32[]{:S(2)}, u32[]{:S(2)}) async-start(f32[16,64,256]{2,1,0:T(8,128)} %shard_map.93), calls=%async_computation.1 | async-start | bytes 2097152 | tf_op jit(solution)/shard_map/all_to_all | solution.py:259
  207.2 1.0 copy-start.2
Sparse Core Ops, SparseCore 0:
  13.8 66.4 all-gather.6
  82.6 77.6 all-gather.4

commit v2 on v1

--- a/solution.py
+++ b/solution.py
@@ -29,8 +29,7 @@
     return one(left[0], right[0]) + (one(left[0], right[1]) + one(left[1], right[0]))
 
 
-def leaf_kernel(listed, odd, m_ref, y_ref, l_ref, u_ref, out_ref, *rest):
-    tops_refs, (yh, yl, yth, ytl, lth, ltl) = rest[:STEPS], rest[STEPS:]
+def leaf_kernel(listed, odd, m_ref, y_ref, l_ref, u_ref, out_ref, tops_ref, yh, yl, yth, ytl, lth, ltl):
     panel = l_ref.shape[1]
     listed_count = y_ref.shape[1] // BLK
 
@@ -55,11 +54,12 @@
             out_ref[pl.ds(start, BLK), :] = renewed[k * BLK : (k + 1) * BLK]
     for s in range(STEPS):
         turned = out_ref[s * panel : (s + 1) * panel, :].T
-        tops_refs[s][...] = turned
+        place_here = slice(s * panel, (s + 1) * panel)
+        tops_ref[:, place_here] = turned
 
         @pl.when(odd[s] == 1)
         def _():
-            tops_refs[s][...] = product3(split(turned), split(u_ref[s]), NN)
+            tops_ref[:, place_here] = product3(split(turned), split(u_ref[s]), NN)
 
 
 def leaf(matrix, leaf_vectors, leaf_factors, tree_vectors, leaf_blocks, odd):
@@ -70,7 +70,7 @@
         leaf_kernel,
         out_shape=(
             jax.ShapeDtypeStruct((rows, columns), jnp.float32),
-            *[jax.ShapeDtypeStruct((columns, panel), jnp.float32)] * steps,
+            jax.ShapeDtypeStruct((columns, steps * panel), jnp.float32),
         ),
         grid_spec=pltpu.PrefetchScalarGridSpec(
             num_scalar_prefetch=2,
@@ -83,7 +83,7 @@
             ],
             out_specs=[
                 pl.BlockSpec((rows, width), lambda c, *_: (0, c)),
-                *[pl.BlockSpec((width, panel), lambda c, *_: (c, 0))] * steps,
+                pl.BlockSpec((width, steps * panel), lambda c, *_: (c, 0)),
             ],
             scratch_shapes=[
                 pltpu.VMEM((steps, leaf_rows, panel), jnp.bfloat16),
@@ -103,10 +103,11 @@
     return row < column, row == column
 
 
-def pack_kernel(odd, own_ref, other_ref, f_ref, *out_refs):
+def pack_kernel(odd, own_ref, other_ref, f_ref, all_ref):
     half = own_ref.shape[1]
     above, on = corner_masks(half)
-    for s, out_ref in enumerate(out_refs):
+    for s in range(STEPS):
+        out_ref = all_ref.at[s]
         out_ref[:half, :] = own_ref[s]
 
         @pl.when(odd[s] == 1)
@@ -124,10 +125,10 @@
 
 def pack(own, other, factors, odd):
     steps, half, panel = own.shape
-    shape = (panel + 8, panel)
+    shape = (steps, panel + 8, panel)
     return pl.pallas_call(
         pack_kernel,
-        out_shape=[jax.ShapeDtypeStruct(shape, jnp.float32)] * steps,
+        out_shape=jax.ShapeDtypeStruct(shape, jnp.float32),
         grid_spec=pltpu.PrefetchScalarGridSpec(
             num_scalar_prefetch=1,
             grid=(1,),
@@ -136,9 +137,133 @@
                 pl.BlockSpec(other.shape, lambda c, *_: (0, 0, 0)),
                 pl.BlockSpec(factors.shape, lambda c, *_: (0, 0, 0)),
             ],
-            out_specs=[pl.BlockSpec(shape, lambda c, *_: (0, 0))] * steps,
+            out_specs=pl.BlockSpec(shape, lambda c, *_: (0, 0, 0)),
         ),
     )(odd, own, other, factors)
+
+
+def chip_at(place, chips):
+    return jnp.where(place < chips // 2, 2 * place, 2 * (chips - 1 - place) + 1)
+
+
+def place_of(chip, chips):
+    return jnp.where(chip % 2 == 0, chip // 2, chips - 1 - chip // 2)
+
+
+def exchange_kernel(
+    count, p_ref, t_ref, g_ref, r_ref, ring_send, ring_recv, pass_send, pass_recv, a2a_send, a2a_recv, own_sem
+):
+    me = lax.axis_index("row")
+    chips = count // 2
+    core = me % 2
+    place = place_of(me // 2, chips)
+
+    def device(offset):
+        return chip_at((place + offset + chips) % chips, chips) * 2 + core
+
+    partner = me + 1 - 2 * core
+    right, left = device(1), device(-1)
+
+    barrier = pltpu.get_barrier_semaphore()
+    for j in range(1, count):
+        pl.semaphore_signal(
+            barrier, inc=1, device_id={"row": (me + j) % count}, device_id_type=pl.DeviceIdType.MESH
+        )
+    pl.semaphore_wait(barrier, count - 1)
+
+    def send(source, target, send_sem, recv_sem, peer):
+        return pltpu.make_async_remote_copy(
+            src_ref=source,
+            dst_ref=target,
+            send_sem=send_sem,
+            recv_sem=recv_sem,
+            device_id={"row": peer},
+            device_id_type=pl.DeviceIdType.MESH,
+        )
+
+    lengths = {(0, 0): chips // 2, (0, 1): chips - 1 - chips // 2}
+    lengths[1, 1], lengths[1, 0] = lengths[0, 0], lengths[0, 1]
+    waits = []
+
+    def hop(s, way, t):
+        origin = device(-t if way == 0 else t)
+        source = p_ref.at[s] if t == 0 else g_ref.at[origin, s]
+        copy = send(
+            source,
+            g_ref.at[origin, s],
+            ring_send.at[s, way, t],
+            ring_recv.at[s, way, t],
+            right if way == 0 else left,
+        )
+        copy.start()
+        waits.append(copy.wait_send)
+        return copy
+
+    def hand(s, slot, source, origin):
+        copy = send(source, g_ref.at[origin, s], pass_send.at[s, slot], pass_recv.at[s, slot], partner)
+        copy.start()
+        waits.append(copy.wait)
+
+    def scatter(j):
+        peer = (me + j) % count
+        copy = send(t_ref.at[peer], r_ref.at[me], a2a_send.at[j - 1], a2a_recv.at[j - 1], peer)
+        copy.start()
+        waits.append(copy.wait)
+
+    flying = {}
+    for s, way in lengths:
+        if lengths[s, way] > 0:
+            flying[s, way] = hop(s, way, 0)
+    for s in range(STEPS):
+        hand(s, 0, p_ref.at[s], me)
+        copy = pltpu.make_async_copy(p_ref.at[s], g_ref.at[me, s], own_sem.at[s])
+        copy.start()
+        waits.append(copy.wait)
+    copy = pltpu.make_async_copy(t_ref.at[me], r_ref.at[me], own_sem.at[STEPS])
+    copy.start()
+    waits.append(copy.wait)
+
+    longest = max(lengths.values())
+    todo = [(j + count // 2 - 1) % (count - 1) + 1 for j in range(count - 1)]
+    share = -(-len(todo) // longest)
+    for t in range(longest):
+        for j in todo[t * share : (t + 1) * share]:
+            scatter(j)
+        for s, way in lengths:
+            if t < lengths[s, way]:
+                flying[s, way].wait_recv()
+                origin = device(-t - 1 if way == 0 else t + 1)
+                if t + 1 < lengths[s, way]:
+                    flying[s, way] = hop(s, way, t + 1)
+                slot = 1 + (t if way == 0 else lengths[s, 0] + t)
+                hand(s, slot, g_ref.at[origin, s], origin)
+    for wait in waits:
+        wait()
+
+
+def exchange(packed, spread):
+    count = spread.shape[0]
+    chips = count // 2
+    dma = pltpu.SemaphoreType.DMA
+    return pl.pallas_call(
+        functools.partial(exchange_kernel, count),
+        out_shape=(
+            jax.ShapeDtypeStruct((count,) + packed.shape, jnp.float32),
+            jax.ShapeDtypeStruct(spread.shape, jnp.float32),
+        ),
+        in_specs=[pl.BlockSpec(memory_space=pltpu.VMEM), pl.BlockSpec(memory_space=pl.ANY)],
+        out_specs=[pl.BlockSpec(memory_space=pl.ANY)] * 2,
+        scratch_shapes=[
+            dma((STEPS, 2, chips)),
+            dma((STEPS, 2, chips)),
+            dma((STEPS, chips)),
+            dma((STEPS, chips)),
+            dma((count - 1,)),
+            dma((count - 1,)),
+            dma((STEPS + 1,)),
+        ],
+        compiler_params=pltpu.CompilerParams(collective_id=0, has_side_effects=True),
+    )(packed, spread)
 
 
 def tree_kernel(upper, lower, x_ref, g_ref, out_ref):
@@ -178,19 +303,22 @@
         out_ref[b] = xb - product3(split(w), u, NT)
 
 
-def tree(spread, reflectors, upper, lower):
-    devices = spread.shape[0]
+def tree(step, spread, reflectors, upper, lower):
+    devices, width, both = spread.shape
+    block = (devices, width, both // STEPS)
     return pl.pallas_call(
         tree_kernel,
-        out_shape=jax.ShapeDtypeStruct(spread.shape, jnp.float32),
+        out_shape=jax.ShapeDtypeStruct(block, jnp.float32),
         grid_spec=pltpu.PrefetchScalarGridSpec(
             num_scalar_prefetch=2,
             grid=(devices - 1,),
             in_specs=[
-                pl.BlockSpec(spread.shape, lambda n, *_: (0, 0, 0)),
-                pl.BlockSpec((2,) + reflectors.shape[1:], lambda n, up, lo: (lo[n] // 2, 0, 0)),
-            ],
-            out_specs=pl.BlockSpec(spread.shape, lambda n, *_: (0, 0, 0)),
+                pl.BlockSpec(block, lambda n, *_: (0, 0, step)),
+                pl.BlockSpec(
+                    (2, None) + reflectors.shape[2:], lambda n, up, lo: (lo[n] // 2, step, 0, 0)
+                ),
+            ],
+            out_specs=pl.BlockSpec(block, lambda n, *_: (0, 0, 0)),
         ),
     )(upper, lower, spread, reflectors)
 
@@ -248,14 +376,14 @@
     asked = lax.dynamic_slice_in_dim(tree_vectors, (1 - core) * half, half, axis=1)
     other = lax.ppermute(asked, "row", [(i, i ^ 1) for i in range(row_count)])
     packed = pack(own, other, tree_factors, odd)
-    reflectors = [lax.all_gather(p, "row") for p in packed]
-    work, *tops = leaf(matrix, leaf_vectors, leaf_factors, tree_vectors, leaf_blocks, odd)
+    work, tops = leaf(matrix, leaf_vectors, leaf_factors, tree_vectors, leaf_blocks, odd)
+    reflectors, spread = exchange(
+        packed, tops.reshape(row_count, columns // row_count, STEPS * panel)
+    )
     uppers, lowers = pairs(row_count)
     for s in range(STEPS):
-        spread = tops[s].reshape(row_count, columns // row_count, panel)
-        spread = lax.all_to_all(spread, "row", 0, 0)
         upper, lower = (uppers + owner[s]) % row_count, (lowers + owner[s]) % row_count
-        done = tree(spread, reflectors[s], upper, lower)
+        done = tree(s, spread, reflectors, upper, lower)
         back = lax.all_to_all(done, "row", 0, 0).reshape(columns, panel)
         work = place(s, back, tree_vectors[s], work, odd[s : s + 1])
     return work

time: 221 us -> 209 us (0.946)
  Pallas kernels: 62.9 us -> 157 us
  blocking collectives: 48.9 us -> 0 us
  waiting for transfers between devices: 68.8 us -> 28.3 us
  between operations: 13.4 us -> 0.04 us
  starting transfers between devices: 17.3 us -> 11.3 us
    pallas_call x3 -> x4, Pallas kernels: 32.9 us -> 127 us  [the longest x1 94.5 us: exchange(): pl.pallas_call(functools.partial(exchange_kernel, count), out_shape=(jax....]
    all_to_all x1 -> x0, blocking collectives: 48.9 us -> none  [shards(): spread = lax.all_to_all(spread, 'row', 0, 0)]
    all_gather x2 -> x0, waiting for transfers between devices: 33 us -> none  [shards(): reflectors = [lax.all_gather(p, 'row') for p in packed]]
    all_to_all x1 -> x0, waiting for transfers between devices: 16.1 us -> none  [shards(): spread = lax.all_to_all(spread, 'row', 0, 0)]
    all_to_all x2, waiting for transfers between devices: 18.9 us -> 28.3 us  [shards(): back = lax.all_to_all(done, 'row', 0, 0).reshape(columns, panel)]
    all_to_all x1 -> x0, starting transfers between devices: 4.89 us -> none  [shards(): spread = lax.all_to_all(spread, 'row', 0, 0)]
  transfers between devices with their start and end apart: 6 -> 3, of which waited for: 3 -> 2; matrix products, arithmetic and copies ran while one was open for 2% -> 3% of each run, Pallas kernels for 25% -> 20%
where the time goes in v2:
time: 209 us; the launch traced here: 206 us
  Pallas kernels  157 us (75%)
  waiting for transfers between devices  28.3 us (14%)
  starting transfers between devices  11.3 us (5%)
  local copies, waits for them, and re-layouts  6.38 us (3%)
  other arithmetic  2.93 us (1%)
    pallas_call x1, Pallas kernels, exchange(): pl.pallas_call(functools.partial(exchange_kernel, count), out_shape=(jax....  94.5 us
    pallas_call x2, Pallas kernels, tree(): pl.pallas_call(tree_kernel, out_shape=jax.ShapeDtypeStruct(block, jnp.flo...  30.1 us
    all_to_all x2, waiting for transfers between devices, shards(): back = lax.all_to_all(done, 'row', 0, 0).reshape(columns, panel)  28.3 us
    pallas_call x1, Pallas kernels, leaf(): pl.pallas_call(leaf_kernel, out_shape=(jax.ShapeDtypeStruct((rows, column...  20.5 us
    all_to_all x2, starting transfers between devices, shards(): back = lax.all_to_all(done, 'row', 0, 0).reshape(columns, panel)  10.6 us
    pallas_call x2, Pallas kernels, place(): pl.pallas_call(place_kernel, out_shape=jax.ShapeDtypeStruct(work.shape, j...  9.47 us
  transfers between devices with their start and end apart: 3, of which 2 were waited for; matrix products, arithmetic and copies ran while one was open for 3% of the time, Pallas kernels for 20%

profile of v2, /device:TPU:11, one launch (start us, length us, event | category | flops | bytes accessed | tf_op | source)
XLA Modules:
  0.0 206.4 jit_solution(980973767795211757)
XLA Ops:
  0.0 0.0 copy-start.5
  0.0 0.0 copy-start.6
  0.0 1.8 constant_dynamic-slice_fusion
  1.8 0.7 collective-permute-start
  2.5 1.1 and_select_fusion.4.odd
  3.6 1.4 fusion.5
  5.0 20.5 %shard_map.92 = (f32[1024,1024]{1,0:T(8,128)}, f32[1024,512]{1,0:T(8,128)}) custom-call(s32[2,5]{1,0:T(2,128)} %listed.1, s32[2]{0:T(128)} %and_select_fusion.4.odd, f32[1024,1024]{1,0:T(8,128)} %m_ref.1, f32[2,640,256]{2,1,0:T(8,128)} %y_ref.1, f32[2,256,256]{2,1,0:T(8,128)} %l_ref.1, f32[2,256,256]{2,1,0:T(8,128)} %u_ref.1), custom_call_target="tpu_custom_call" | custom-call | tf_op jit(solution)/shard_map/pallas_call | solution.py:69
  25.5 0.0 copy-done.5
  25.5 0.0 copy-done.6
  25.5 1.8 and_select_fusion
  27.3 0.0 collective-permute-done.other_ref
  27.3 0.0 copy-start.3
  27.3 0.7 copy-done.3
  28.0 2.9 %shard_map.91.p_ref = f32[2,264,256]{2,1,0:T(8,128)} custom-call(s32[2]{0:T(128)} %and_select_fusion.4.odd, f32[2,128,256]{2,1,0:T(8,128)} %get-tuple-element.16.own_ref, f32[2,128,256]{2,1,0:T(8,128)} %copy-done.3, f32[2,256,256]{2,1,0:T(8,128)} %f_ref.1), custom_call_target="tpu_custom_call" | custom-call | tf_op jit(solution)/shard_map/pallas_call | solution.py:129
  30.9 94.5 %shard_map.93 = (f32[16,2,264,256]{3,2,1,0:T(8,128)}, f32[16,64,512]{2,1,0:T(8,128)}) custom-call(f32[2,264,256]{2,1,0:T(8,128)} %shard_map.91.p_ref, f32[16,64,512]{2,1,0:T(8,128)} %bitcast.11), custom_call_target="tpu_custom_call" | custom-call | tf_op jit(solution)/shard_map/pallas_call | solution.py:248
  125.4 15.0 %shard_map.95 = f32[16,64,256]{2,1,0:T(8,128)} custom-call(s32[15]{0:T(128)} %get-tuple-element.26.upper, s32[15]{0:T(128)} %get-tuple-element.17.lower, f32[16,64,512]{2,1,0:T(8,128)} %get-tuple-element.10.x_ref, f32[16,2,264,256]{3,2,1,0:T(8,128)} %get-tuple-element.11.g_ref), custom_call_target="tpu_custom_call" | custom-call | tf_op jit(solution)/shard_map/pallas_call | solution.py:309
  140.3 5.9 %all-to-all-start.1 = ((f32[16,64,256]{2,1,0:T(8,128)}), f32[16,64,256]{2,1,0:T(8,128)S(1)}, u32[]{:S(2)}, u32[]{:S(2)}) async-start(f32[16,64,256]{2,1,0:T(8,128)} %shard_map.95), calls=%async_computation.1 | async-start | bytes 2097152 | tf_op jit(solution)/shard_map/all_to_all | solution.py:387
  146.2 0.0 copy-start.4
  146.2 0.0 copy-start
  146.2 15.1 %shard_map.94 = f32[16,64,256]{2,1,0:T(8,128)} custom-call(s32[15]{0:T(128)} %get-tuple-element.25.upper, s32[15]{0:T(128)} %get-tuple-element.18.lower, f32[16,64,512]{2,1,0:T(8,128)} %get-tuple-element.10.x_ref, f32[16,2,264,256]{3,2,1,0:T(8,128)} %get-tuple-element.11.g_ref), custom_call_target="tpu_custom_call" | custom-call | tf_op jit(solution)/shard_map/pallas_call | solution.py:309
  161.4 9.8 %all-to-all-done.1 = f32[16,64,256]{2,1,0:T(8,128)S(1)} async-done(((f32[16,64,256]{2,1,0:T(8,128)}), f32[16,64,256]{2,1,0:T(8,128)S(1)}, u32[]{:S(2)}, u32[]{:S(2)}) %all-to-all-start.1) | async-done | bytes 1048608 | tf_op jit(solution)/shard_map/all_to_all | solution.py:387
  171.2 0.0 copy-start.1
  171.2 4.7 %all-to-all-start = ((f32[16,64,256]{2,1,0:T(8,128)}), f32[16,64,256]{2,1,0:T(8,128)S(1)}, u32[]{:S(2)}, u32[]{:S(2)}) async-start(f32[16,64,256]{2,1,0:T(8,128)} %shard_map.94), calls=%async_computation | async-start | bytes 2097152 | tf_op jit(solution)/shard_map/all_to_all | solution.py:387
  175.9 0.0 copy-done.4
  175.9 0.6 fusion.6
  176.5 0.0 copy-done
  176.5 0.9 slice_bitcast_fusion
  177.4 0.0 copy-done.1
  177.4 4.9 %shard_map.96.work_ref = f32[1024,1024]{1,0:T(8,128)} custom-call(s32[1]{0:T(128)} %get-tuple-element.23.odd, f32[1024,256]{1,0:T(8,128)} %bitcast.9, f32[256,256]{1,0:T(8,128)} %get-tuple-element.13.u_ref, f32[1024,1024]{1,0:T(8,128)} %get-tuple-element.12.work_ref), custom_call_target="tpu_custom_call", output_to_operand_aliasing={{}: (3, {})} | custom-call | tf_op jit(solution)/shard_map/pallas_call | solution.py:339
  182.3 18.5 %all-to-all-done = f32[16,64,256]{2,1,0:T(8,128)S(1)} async-done(((f32[16,64,256]{2,1,0:T(8,128)}), f32[16,64,256]{2,1,0:T(8,128)S(1)}, u32[]{:S(2)}, u32[]{:S(2)}) %all-to-all-start) | async-done | bytes 1048608 | tf_op jit(solution)/shard_map/all_to_all | solution.py:387
  200.8 1.0 copy-done.2
  201.8 4.6 %shard_map.97 = f32[1024,1024]{1,0:T(8,128)} custom-call(s32[1]{0:T(128)} %get-tuple-element.24.odd, f32[1024,256]{1,0:T(8,128)} %bitcast.10, f32[256,256]{1,0:T(8,128)} %get-tuple-element.14.u_ref, f32[1024,1024]{1,0:T(8,128)} %shard_map.96.work_ref), custom_call_target="tpu_custom_call", output_to_operand_aliasing={{}: (3, {})} | custom-call | tf_op jit(solution)/shard_map/pallas_call | solution.py:339
  (1 shorter events, 0.0 us)
Async XLA Ops:
  0.0 25.5 %copy-start.5 = (s32[15]{0:T(128)S(1)}, s32[15]{0:T(128)}, u32[]{:S(2)}) copy-start(s32[15]{0:T(128)} %constant.65.clone) | copy-start | bytes 184
  0.0 25.5 %copy-start.6 = (s32[15]{0:T(128)S(1)}, s32[15]{0:T(128)}, u32[]{:S(2)}) copy-start(s32[15]{0:T(128)} %constant.64.clone) | copy-start | bytes 184
  1.8 25.4 %collective-permute-start = (f32[2,128,256]{2,1,0:T(8,128)S(1)}, f32[2,128,256]{2,1,0:T(8,128)S(1)}, u32[]{:S(2)}, u32[]{:S(2)}) collective-permute-start(f32[2,128,256]{2,1,0:T(8,128)S(1)} %get-tuple-element.15), channel_id=1, source_target_pairs={{0,1},{1,0},{2,3},{3,2},{4,5},{5,4},{6,7},{7,6},{8,9},{9,8},{10,11... | collective-permute-start | bytes 786440 | tf_op jit(solution)/shard_map/ppermute | solution.py:377
  27.3 0.7 copy-start.3
  140.3 30.8 %all-to-all-start.1 = ((f32[16,64,256]{2,1,0:T(8,128)}), f32[16,64,256]{2,1,0:T(8,128)S(1)}, u32[]{:S(2)}, u32[]{:S(2)}) async-start(f32[16,64,256]{2,1,0:T(8,128)} %shard_map.95), calls=%async_computation.1 | async-start | bytes 2097152 | tf_op jit(solution)/shard_map/all_to_all | solution.py:387
  146.2 29.7 %copy-start.4 = (s32[2]{0:T(128)S(1)}, s32[2]{0:T(128)}, u32[]{:S(2)}) copy-start(s32[2]{0:T(128)} %and_select_fusion.4.odd) | copy-start | bytes 28
  146.2 30.3 %copy-start = (f32[2,256,256]{2,1,0:T(8,128)S(1)}, f32[2,256,256]{2,1,0:T(8,128)}, u32[]{:S(2)}) copy-start(f32[2,256,256]{2,1,0:T(8,128)} %u_ref.1) | copy-start | bytes 1572868
  171.2 6.3 %copy-start.1 = (f32[16,64,256]{2,1,0:T(8,128)}, f32[16,64,256]{2,1,0:T(8,128)S(1)}, u32[]{:S(2)}) copy-start(f32[16,64,256]{2,1,0:T(8,128)S(1)} %all-to-all-done.1) | copy-start | bytes 3145732
  171.2 29.7 %all-to-all-start = ((f32[16,64,256]{2,1,0:T(8,128)}), f32[16,64,256]{2,1,0:T(8,128)S(1)}, u32[]{:S(2)}, u32[]{:S(2)}) async-start(f32[16,64,256]{2,1,0:T(8,128)} %shard_map.94), calls=%async_computation | async-start | bytes 2097152 | tf_op jit(solution)/shard_map/all_to_all | solution.py:387
  200.8 1.0 copy-start.2

commit v3 on v2

--- a/solution.py
+++ b/solution.py
@@ -27,74 +27,6 @@
         return lax.dot_general(a, b, dims, preferred_element_type=jnp.float32)
 
     return one(left[0], right[0]) + (one(left[0], right[1]) + one(left[1], right[0]))
-
-
-def leaf_kernel(listed, odd, m_ref, y_ref, l_ref, u_ref, out_ref, tops_ref, yh, yl, yth, ytl, lth, ltl):
-    panel = l_ref.shape[1]
-    listed_count = y_ref.shape[1] // BLK
-
-    @pl.when(pl.program_id(0) == 0)
-    def _():
-        for s in range(STEPS):
-            high, low = split(y_ref[s])
-            yh[s], yl[s] = high, low
-            high, low = split(y_ref[s].T)
-            yth[s], ytl[s] = high, low
-            high, low = split(l_ref[s].T)
-            lth[s], ltl[s] = high, low
-
-    out_ref[...] = m_ref[...]
-    for s in range(STEPS):
-        starts = [pl.multiple_of(listed[s, k] * BLK, BLK) for k in range(listed_count)]
-        gathered = jnp.concatenate([out_ref[pl.ds(start, BLK), :] for start in starts], axis=0)
-        projected = product3((yth[s], ytl[s]), split(gathered), NN)
-        update = product3((lth[s], ltl[s]), split(projected), NN)
-        renewed = gathered - product3((yh[s], yl[s]), split(update), NN)
-        for k, start in enumerate(starts):
-            out_ref[pl.ds(start, BLK), :] = renewed[k * BLK : (k + 1) * BLK]
-    for s in range(STEPS):
-        turned = out_ref[s * panel : (s + 1) * panel, :].T
-        place_here = slice(s * panel, (s + 1) * panel)
-        tops_ref[:, place_here] = turned
-
-        @pl.when(odd[s] == 1)
-        def _():
-            tops_ref[:, place_here] = product3(split(turned), split(u_ref[s]), NN)
-
-
-def leaf(matrix, leaf_vectors, leaf_factors, tree_vectors, leaf_blocks, odd):
-    rows, columns = matrix.shape
-    width = COLS_PER_LEAF
-    steps, leaf_rows, panel = leaf_vectors.shape
-    return pl.pallas_call(
-        leaf_kernel,
-        out_shape=(
-            jax.ShapeDtypeStruct((rows, columns), jnp.float32),
-            jax.ShapeDtypeStruct((columns, steps * panel), jnp.float32),
-        ),
-        grid_spec=pltpu.PrefetchScalarGridSpec(
-            num_scalar_prefetch=2,
-            grid=(columns // width,),
-            in_specs=[
-                pl.BlockSpec((rows, width), lambda c, *_: (0, c)),
-                pl.BlockSpec(leaf_vectors.shape, lambda c, *_: (0, 0, 0)),
-                pl.BlockSpec(leaf_factors.shape, lambda c, *_: (0, 0, 0)),
-                pl.BlockSpec(tree_vectors.shape, lambda c, *_: (0, 0, 0)),
-            ],
-            out_specs=[
-                pl.BlockSpec((rows, width), lambda c, *_: (0, c)),
-                pl.BlockSpec((width, steps * panel), lambda c, *_: (c, 0)),
-            ],
-            scratch_shapes=[
-                pltpu.VMEM((steps, leaf_rows, panel), jnp.bfloat16),
-                pltpu.VMEM((steps, leaf_rows, panel), jnp.bfloat16),
-                pltpu.VMEM((steps, panel, leaf_rows), jnp.bfloat16),
-                pltpu.VMEM((steps, panel, leaf_rows), jnp.bfloat16),
-                pltpu.VMEM((steps, panel, panel), jnp.bfloat16),
-                pltpu.VMEM((steps, panel, panel), jnp.bfloat16),
-            ],
-        ),
-    )(leaf_blocks, odd, matrix, leaf_vectors, leaf_factors, tree_vectors)
 
 
 def corner_masks(half):
@@ -150,11 +82,58 @@
     return jnp.where(chip % 2 == 0, chip // 2, chips - 1 - chip // 2)
 
 
-def exchange_kernel(
-    count, p_ref, t_ref, g_ref, r_ref, ring_send, ring_recv, pass_send, pass_recv, a2a_send, a2a_recv, own_sem
-):
+def leaf_block(listed, odd, m_ref, u_ref, out_ref, tops_ref, first, parts):
+    yh, yl, yth, ytl, lth, ltl, uh, ul = parts
+    panel = u_ref.shape[1]
+    width = out_ref.shape[1]
+    block_count = out_ref.shape[0] // BLK
+    listed_count = yh.shape[1] // BLK
+    panel_blocks = panel // BLK
+    out_ref[...] = m_ref[...]
+    for s in range(STEPS):
+        inner = range((s + 1) * panel_blocks, block_count - 1)
+        numbers = {
+            k: jnp.full((BLK, width), listed[s, k], jnp.int32)
+            for k in range(panel_blocks, listed_count - 1)
+        }
+        taken = [out_ref[s * panel : (s + 1) * panel, :]]
+        for number in numbers.values():
+            block_rows = jnp.zeros((BLK, width), jnp.float32)
+            for block in inner:
+                here = out_ref[block * BLK : (block + 1) * BLK, :]
+                block_rows = jnp.where(number == block, here, block_rows)
+            taken.append(block_rows)
+        taken.append(out_ref[(block_count - 1) * BLK :, :])
+        gathered = jnp.concatenate(taken, axis=0)
+        projected = product3((yth[s], ytl[s]), split(gathered), NN)
+        update = product3((lth[s], ltl[s]), split(projected), NN)
+        change = product3((yh[s], yl[s]), split(update), NN)
+        pieces = [change[k * BLK : (k + 1) * BLK] for k in range(listed_count)]
+        fixed = [(s * panel_blocks + k, pieces[k]) for k in range(panel_blocks)]
+        for block, piece in fixed + [(block_count - 1, pieces[-1])]:
+            out_ref[block * BLK : (block + 1) * BLK, :] -= piece
+        for block in inner:
+            amount = jnp.zeros((BLK, width), jnp.float32)
+            for k, number in numbers.items():
+                amount = jnp.where(number == block, pieces[k], amount)
+            out_ref[block * BLK : (block + 1) * BLK, :] -= amount
+    for s in range(STEPS):
+        turned = out_ref[s * panel : (s + 1) * panel, :].T
+        projected = product3(split(turned), (uh[s], ul[s]), NN)
+        flag = jnp.full(turned.shape, odd[s], jnp.int32)
+        tops_ref[pl.ds(first, width), s * panel : (s + 1) * panel] = jnp.where(
+            flag == 1, projected, turned
+        )
+
+
+def exchange_kernel(count, listed, odd, m_ref, y_ref, l_ref, u_ref, p_ref, work_ref, g_ref, r_ref, *rest):
+    parts = rest[:8]
+    t_ref, ring_send, ring_recv, pass_send, pass_recv, a2a_send, a2a_recv, own_sem = rest[8:]
+    turn = pl.program_id(0)
+    turns = t_ref.shape[0] // m_ref.shape[1]
     me = lax.axis_index("row")
     chips = count // 2
+    share = t_ref.shape[0] // count
     core = me % 2
     place = place_of(me // 2, chips)
 
@@ -164,14 +143,7 @@
     partner = me + 1 - 2 * core
     right, left = device(1), device(-1)
 
-    barrier = pltpu.get_barrier_semaphore()
-    for j in range(1, count):
-        pl.semaphore_signal(
-            barrier, inc=1, device_id={"row": (me + j) % count}, device_id_type=pl.DeviceIdType.MESH
-        )
-    pl.semaphore_wait(barrier, count - 1)
-
-    def send(source, target, send_sem, recv_sem, peer):
+    def remote(source, target, send_sem, recv_sem, peer):
         return pltpu.make_async_remote_copy(
             src_ref=source,
             dst_ref=target,
@@ -183,87 +155,155 @@
 
     lengths = {(0, 0): chips // 2, (0, 1): chips - 1 - chips // 2}
     lengths[1, 1], lengths[1, 0] = lengths[0, 0], lengths[0, 1]
-    waits = []
+    longest = max(lengths.values())
 
     def hop(s, way, t):
         origin = device(-t if way == 0 else t)
         source = p_ref.at[s] if t == 0 else g_ref.at[origin, s]
-        copy = send(
+        return remote(
             source,
             g_ref.at[origin, s],
             ring_send.at[s, way, t],
             ring_recv.at[s, way, t],
             right if way == 0 else left,
         )
-        copy.start()
-        waits.append(copy.wait_send)
-        return copy
-
-    def hand(s, slot, source, origin):
-        copy = send(source, g_ref.at[origin, s], pass_send.at[s, slot], pass_recv.at[s, slot], partner)
-        copy.start()
-        waits.append(copy.wait)
+
+    def hand(s, way, t):
+        if t < 0:
+            return remote(
+                p_ref.at[s], g_ref.at[me, s], pass_send.at[s, 0], pass_recv.at[s, 0], partner
+            )
+        origin = device(-t - 1 if way == 0 else t + 1)
+        slot = 1 + (t if way == 0 else lengths[s, 0] + t)
+        piece = g_ref.at[origin, s]
+        return remote(piece, piece, pass_send.at[s, slot], pass_recv.at[s, slot], partner)
+
+    def columns_of(peer):
+        return t_ref.at[pl.ds(pl.multiple_of(peer * share, 8), share), :]
 
     def scatter(j):
         peer = (me + j) % count
-        copy = send(t_ref.at[peer], r_ref.at[me], a2a_send.at[j - 1], a2a_recv.at[j - 1], peer)
-        copy.start()
-        waits.append(copy.wait)
-
-    flying = {}
-    for s, way in lengths:
-        if lengths[s, way] > 0:
-            flying[s, way] = hop(s, way, 0)
-    for s in range(STEPS):
-        hand(s, 0, p_ref.at[s], me)
-        copy = pltpu.make_async_copy(p_ref.at[s], g_ref.at[me, s], own_sem.at[s])
-        copy.start()
-        waits.append(copy.wait)
-    copy = pltpu.make_async_copy(t_ref.at[me], r_ref.at[me], own_sem.at[STEPS])
-    copy.start()
-    waits.append(copy.wait)
-
-    longest = max(lengths.values())
-    todo = [(j + count // 2 - 1) % (count - 1) + 1 for j in range(count - 1)]
-    share = -(-len(todo) // longest)
-    for t in range(longest):
-        for j in todo[t * share : (t + 1) * share]:
-            scatter(j)
+        return remote(columns_of(peer), r_ref.at[me], a2a_send.at[j - 1], a2a_recv.at[j - 1], peer)
+
+    def keep(s):
+        return pltpu.make_async_copy(p_ref.at[s], g_ref.at[me, s], own_sem.at[s])
+
+    def keep_columns():
+        return pltpu.make_async_copy(columns_of(me), r_ref.at[me], own_sem.at[STEPS])
+
+    def advance(t):
         for s, way in lengths:
             if t < lengths[s, way]:
-                flying[s, way].wait_recv()
-                origin = device(-t - 1 if way == 0 else t + 1)
+                hop(s, way, t).wait_recv()
                 if t + 1 < lengths[s, way]:
-                    flying[s, way] = hop(s, way, t + 1)
-                slot = 1 + (t if way == 0 else lengths[s, 0] + t)
-                hand(s, slot, g_ref.at[origin, s], origin)
-    for wait in waits:
-        wait()
-
-
-def exchange(packed, spread):
-    count = spread.shape[0]
+                    hop(s, way, t + 1).start()
+                hand(s, way, t).start()
+
+    @pl.when(turn == 0)
+    def _():
+        barrier = pltpu.get_barrier_semaphore()
+        for j in range(1, count):
+            pl.semaphore_signal(
+                barrier,
+                inc=1,
+                device_id={"row": (me + j) % count},
+                device_id_type=pl.DeviceIdType.MESH,
+            )
+        pl.semaphore_wait(barrier, count - 1)
+        for s, way in lengths:
+            if lengths[s, way] > 0:
+                hop(s, way, 0).start()
+        for s in range(STEPS):
+            hand(s, 0, -1).start()
+            keep(s).start()
+        yh, yl, yth, ytl, lth, ltl, uh, ul = parts
+        for s in range(STEPS):
+            yh[s], yl[s] = split(y_ref[s])
+            yth[s], ytl[s] = split(y_ref[s].T)
+            lth[s], ltl[s] = split(l_ref[s].T)
+            uh[s], ul[s] = split(u_ref[s])
+
+    first = pl.multiple_of(turn * m_ref.shape[1], m_ref.shape[1])
+    leaf_block(listed, odd, m_ref, u_ref, work_ref, t_ref, first, parts)
+
+    early = min(turns - 1, longest)
+    for t in range(early):
+
+        @pl.when(turn == t)
+        def _():
+            advance(t)
+
+    @pl.when(turn == turns - 1)
+    def _():
+        todo = [(j + count // 2 - 1) % (count - 1) + 1 for j in range(count - 1)]
+        rounds = max(longest - early, 1)
+        size = -(-len(todo) // rounds)
+        keep_columns().start()
+        for t in range(rounds):
+            for j in todo[t * size : (t + 1) * size]:
+                scatter(j).start()
+            advance(early + t)
+        for s, way in lengths:
+            for t in range(lengths[s, way]):
+                hop(s, way, t).wait_send()
+                hand(s, way, t).wait()
+        for s in range(STEPS):
+            hand(s, 0, -1).wait()
+            keep(s).wait()
+        keep_columns().wait()
+        for j in todo:
+            scatter(j).wait()
+
+
+def exchange(count, matrix, leaf_vectors, leaf_factors, tree_vectors, packed, leaf_blocks, odd):
+    rows, columns = matrix.shape
+    width = COLS_PER_LEAF
+    steps, leaf_rows, panel = leaf_vectors.shape
     chips = count // 2
     dma = pltpu.SemaphoreType.DMA
+    half_type = jnp.bfloat16
+
+    def whole(array):
+        return pl.BlockSpec(array.shape, lambda c, *_: (0, 0, 0))
+
     return pl.pallas_call(
         functools.partial(exchange_kernel, count),
         out_shape=(
+            jax.ShapeDtypeStruct((rows, columns), jnp.float32),
             jax.ShapeDtypeStruct((count,) + packed.shape, jnp.float32),
-            jax.ShapeDtypeStruct(spread.shape, jnp.float32),
-        ),
-        in_specs=[pl.BlockSpec(memory_space=pltpu.VMEM), pl.BlockSpec(memory_space=pl.ANY)],
-        out_specs=[pl.BlockSpec(memory_space=pl.ANY)] * 2,
-        scratch_shapes=[
-            dma((STEPS, 2, chips)),
-            dma((STEPS, 2, chips)),
-            dma((STEPS, chips)),
-            dma((STEPS, chips)),
-            dma((count - 1,)),
-            dma((count - 1,)),
-            dma((STEPS + 1,)),
-        ],
+            jax.ShapeDtypeStruct((count, columns // count, steps * panel), jnp.float32),
+        ),
+        grid_spec=pltpu.PrefetchScalarGridSpec(
+            num_scalar_prefetch=2,
+            grid=(columns // width,),
+            in_specs=[
+                pl.BlockSpec((rows, width), lambda c, *_: (0, c)),
+                whole(leaf_vectors),
+                whole(leaf_factors),
+                whole(tree_vectors),
+                whole(packed),
+            ],
+            out_specs=[
+                pl.BlockSpec((rows, width), lambda c, *_: (0, c)),
+                pl.BlockSpec(memory_space=pl.ANY),
+                pl.BlockSpec(memory_space=pl.ANY),
+            ],
+            scratch_shapes=[
+                *[pltpu.VMEM((steps, leaf_rows, panel), half_type)] * 2,
+                *[pltpu.VMEM((steps, panel, leaf_rows), half_type)] * 2,
+                *[pltpu.VMEM((steps, panel, panel), half_type)] * 4,
+                pltpu.VMEM((columns, steps * panel), jnp.float32),
+                dma((steps, 2, chips)),
+                dma((steps, 2, chips)),
+                dma((steps, chips)),
+                dma((steps, chips)),
+                dma((count - 1,)),
+                dma((count - 1,)),
+                dma((steps + 1,)),
+            ],
+        ),
         compiler_params=pltpu.CompilerParams(collective_id=0, has_side_effects=True),
-    )(packed, spread)
+    )(leaf_blocks, odd, matrix, leaf_vectors, leaf_factors, tree_vectors, packed)
 
 
 def tree_kernel(upper, lower, x_ref, g_ref, out_ref):
@@ -376,9 +416,8 @@
     asked = lax.dynamic_slice_in_dim(tree_vectors, (1 - core) * half, half, axis=1)
     other = lax.ppermute(asked, "row", [(i, i ^ 1) for i in range(row_count)])
     packed = pack(own, other, tree_factors, odd)
-    work, tops = leaf(matrix, leaf_vectors, leaf_factors, tree_vectors, leaf_blocks, odd)
-    reflectors, spread = exchange(
-        packed, tops.reshape(row_count, columns // row_count, STEPS * panel)
+    work, reflectors, spread = exchange(
+        row_count, matrix, leaf_vectors, leaf_factors, tree_vectors, packed, leaf_blocks, odd
     )
     uppers, lowers = pairs(row_count)
     for s in range(STEPS):

time: 209 us -> 195 us (0.933)
  Pallas kernels: 157 us -> 136 us
  local copies, waits for them, and re-layouts: 6.38 us -> 11.1 us
  starting transfers between devices: 11.3 us -> 14.2 us
    pallas_call x1 -> x0, Pallas kernels: 20.5 us -> none  [leaf(): pl.pallas_call(leaf_kernel, out_shape=(jax.ShapeDtypeStruct((rows, column...]
    unnamed x14 -> x11, local copies, waits for them, and re-layouts: 1.7 us -> 6.47 us
    all_to_all x2, starting transfers between devices: 10.6 us -> 13.6 us  [shards(): back = lax.all_to_all(done, 'row', 0, 0).reshape(columns, panel)]
  transfers between devices with their start and end apart: 3 -> 3, of which waited for: 2 -> 2; matrix products, arithmetic and copies ran while one was open for 3% -> 3% of each run, Pallas kernels for 20% -> 10%
where the time goes in v3:
time: 195 us; the launch traced here: 194 us
  Pallas kernels  136 us (70%)
  waiting for transfers between devices  28.7 us (15%)
  starting transfers between devices  14.2 us (7%)
  local copies, waits for them, and re-layouts  11.1 us (6%)
  other arithmetic  3.74 us (2%)
    pallas_call x1, Pallas kernels, exchange(): pl.pallas_call(functools.partial(exchange_kernel, count), out_shape=(jax....  93.4 us
    pallas_call x2, Pallas kernels, tree(): pl.pallas_call(tree_kernel, out_shape=jax.ShapeDtypeStruct(block, jnp.flo...  30 us
    all_to_all x2, waiting for transfers between devices, shards(): back = lax.all_to_all(done, 'row', 0, 0).reshape(columns, panel)  28.7 us
    all_to_all x2, starting transfers between devices, shards(): back = lax.all_to_all(done, 'row', 0, 0).reshape(columns, panel)  13.6 us
    pallas_call x2, Pallas kernels, place(): pl.pallas_call(place_kernel, out_shape=jax.ShapeDtypeStruct(work.shape, j...  9.55 us
    unnamed x11, local copies, waits for them, and re-layouts  6.47 us
  transfers between devices with their start and end apart: 3, of which 2 were waited for; matrix products, arithmetic and copies ran while one was open for 3% of the time, Pallas kernels for 10%

profile of v3, /device:TPU:11, one launch (start us, length us, event | category | flops | bytes accessed | tf_op | source)
XLA Modules:
  0.0 193.6 jit_solution(11185171577882285526)
XLA Ops:
  0.0 1.8 constant_dynamic-slice_fusion
  1.8 0.7 collective-permute-start
  2.4 1.2 and_select_fusion.4.odd
  3.6 1.4 fusion.5
  5.0 2.6 %and_select_fusion = (s32[15]{0:T(128)}, s32[15]{0:T(128)}, s32[15]{0:T(128)}, s32[15]{0:T(128)}) fusion(s32[15]{0:T(128)} %constant.65.clone, s32[]{:T(128)} %bitcast.3, s32[]{:T(128)} %bitcast, s32[15]{0:T(128)} %constant.64.clone), kind=kLoop, calls=%fused_computation.12 | loop fusion | flops 720 | bytes 368 | tf_op jit(solution)/shard_map/jit(remainder)/select_n | solution.py:424
  7.6 0.0 collective-permute-done.other_ref
  7.6 0.0 copy-start.3
  7.6 0.7 copy-done.3
  8.3 2.9 %shard_map.91.p_ref = f32[2,264,256]{2,1,0:T(8,128)} custom-call(s32[2]{0:T(128)} %and_select_fusion.4.odd, f32[2,128,256]{2,1,0:T(8,128)} %get-tuple-element.14.own_ref, f32[2,128,256]{2,1,0:T(8,128)} %copy-done.3, f32[2,256,256]{2,1,0:T(8,128)} %f_ref.1), custom_call_target="tpu_custom_call" | custom-call | tf_op jit(solution)/shard_map/pallas_call | solution.py:61
  11.2 93.4 %shard_map.92 = (f32[1024,1024]{1,0:T(8,128)}, f32[16,2,264,256]{3,2,1,0:T(8,128)}, f32[16,64,512]{2,1,0:T(8,128)}) custom-call(s32[2,5]{1,0:T(2,128)} %listed.1, s32[2]{0:T(128)} %and_select_fusion.4.odd, f32[1024,1024]{1,0:T(8,128)} %m_ref.1, f32[2,640,256]{2,1,0:T(8,128)} %y_ref.1, f32[2,256,256]{2,1,0:T(8,128)} %l_ref.1, f32[2,256,256]{2,1,0:T(8,128)} %u_ref.1, ...), custom_call_target="tpu_custom_call" | custom-call | tf_op jit(solution)/shard_map/pallas_call | solution.py:269
  104.5 15.0 %shard_map.94 = f32[16,64,256]{2,1,0:T(8,128)} custom-call(s32[15]{0:T(128)} %get-tuple-element.24.upper, s32[15]{0:T(128)} %get-tuple-element.15.lower, f32[16,64,512]{2,1,0:T(8,128)} %get-tuple-element.8.x_ref, f32[16,2,264,256]{3,2,1,0:T(8,128)} %get-tuple-element.9.g_ref), custom_call_target="tpu_custom_call" | custom-call | tf_op jit(solution)/shard_map/pallas_call | solution.py:349
  119.5 8.8 %all-to-all-start.1 = ((f32[16,64,256]{2,1,0:T(8,128)}), f32[16,64,256]{2,1,0:T(8,128)S(1)}, u32[]{:S(2)}, u32[]{:S(2)}) async-start(f32[16,64,256]{2,1,0:T(8,128)} %shard_map.94), calls=%async_computation.1 | async-start | bytes 2097152 | tf_op jit(solution)/shard_map/all_to_all | solution.py:426
  128.3 0.0 copy-start.4
  128.3 0.0 copy-start
  128.3 15.1 %shard_map.93 = f32[16,64,256]{2,1,0:T(8,128)} custom-call(s32[15]{0:T(128)} %get-tuple-element.23.upper, s32[15]{0:T(128)} %get-tuple-element.16.lower, f32[16,64,512]{2,1,0:T(8,128)} %get-tuple-element.8.x_ref, f32[16,2,264,256]{3,2,1,0:T(8,128)} %get-tuple-element.9.g_ref), custom_call_target="tpu_custom_call" | custom-call | tf_op jit(solution)/shard_map/pallas_call | solution.py:349
  143.4 9.8 %all-to-all-done.1 = f32[16,64,256]{2,1,0:T(8,128)S(1)} async-done(((f32[16,64,256]{2,1,0:T(8,128)}), f32[16,64,256]{2,1,0:T(8,128)S(1)}, u32[]{:S(2)}, u32[]{:S(2)}) %all-to-all-start.1) | async-done | bytes 1048608 | tf_op jit(solution)/shard_map/all_to_all | solution.py:426
  153.2 0.0 copy-start.1
  153.2 4.8 %all-to-all-start = ((f32[16,64,256]{2,1,0:T(8,128)}), f32[16,64,256]{2,1,0:T(8,128)S(1)}, u32[]{:S(2)}, u32[]{:S(2)}) async-start(f32[16,64,256]{2,1,0:T(8,128)} %shard_map.93), calls=%async_computation | async-start | bytes 2097152 | tf_op jit(solution)/shard_map/all_to_all | solution.py:426
  158.0 0.0 copy-done.4
  158.0 0.6 fusion.6
  158.6 0.0 copy-done
  158.6 0.9 slice_bitcast_fusion
  159.4 0.0 copy-done.1
  159.4 4.6 %shard_map.95.work_ref = f32[1024,1024]{1,0:T(8,128)} custom-call(s32[1]{0:T(128)} %get-tuple-element.21.odd, f32[1024,256]{1,0:T(8,128)} %bitcast.8, f32[256,256]{1,0:T(8,128)} %get-tuple-element.11.u_ref, f32[1024,1024]{1,0:T(8,128)} %get-tuple-element.10.work_ref), custom_call_target="tpu_custom_call", output_to_operand_aliasing={{}: (3, {})} | custom-call | tf_op jit(solution)/shard_map/pallas_call | solution.py:379
  164.0 18.9 %all-to-all-done = f32[16,64,256]{2,1,0:T(8,128)S(1)} async-done(((f32[16,64,256]{2,1,0:T(8,128)}), f32[16,64,256]{2,1,0:T(8,128)S(1)}, u32[]{:S(2)}, u32[]{:S(2)}) %all-to-all-start) | async-done | bytes 1048608 | tf_op jit(solution)/shard_map/all_to_all | solution.py:426
  182.9 0.0 copy-start.2
  182.9 1.0 copy-done.2
  183.9 4.9 %shard_map.96 = f32[1024,1024]{1,0:T(8,128)} custom-call(s32[1]{0:T(128)} %get-tuple-element.22.odd, f32[1024,256]{1,0:T(8,128)} %bitcast.9, f32[256,256]{1,0:T(8,128)} %get-tuple-element.12.u_ref, f32[1024,1024]{1,0:T(8,128)} %shard_map.95.work_ref), custom_call_target="tpu_custom_call", output_to_operand_aliasing={{}: (3, {})} | custom-call | tf_op jit(solution)/shard_map/pallas_call | solution.py:379
  188.8 4.8 %copy.15 = f32[1024,1024]{1,0:T(8,128)} copy(f32[1024,1024]{1,0:T(8,128)} %shard_map.96) | data formatting | bytes 8388608
Async XLA Ops:
  1.8 5.8 %collective-permute-start = (f32[2,128,256]{2,1,0:T(8,128)S(1)}, f32[2,128,256]{2,1,0:T(8,128)S(1)}, u32[]{:S(2)}, u32[]{:S(2)}) collective-permute-start(f32[2,128,256]{2,1,0:T(8,128)S(1)} %get-tuple-element.13), channel_id=1, source_target_pairs={{0,1},{1,0},{2,3},{3,2},{4,5},{5,4},{6,7},{7,6},{8,9},{9,8},{10,11... | collective-permute-start | bytes 786440 | tf_op jit(solution)/shard_map/ppermute | solution.py:417
  7.6 0.7 copy-start.3
  119.5 33.7 %all-to-all-start.1 = ((f32[16,64,256]{2,1,0:T(8,128)}), f32[16,64,256]{2,1,0:T(8,128)S(1)}, u32[]{:S(2)}, u32[]{:S(2)}) async-start(f32[16,64,256]{2,1,0:T(8,128)} %shard_map.94), calls=%async_computation.1 | async-start | bytes 2097152 | tf_op jit(solution)/shard_map/all_to_all | solution.py:426
  128.3 29.7 %copy-start.4 = (s32[2]{0:T(128)S(1)}, s32[2]{0:T(128)}, u32[]{:S(2)}) copy-start(s32[2]{0:T(128)} %and_select_fusion.4.odd) | copy-start | bytes 28
  128.3 30.3 %copy-start = (f32[2,256,256]{2,1,0:T(8,128)S(1)}, f32[2,256,256]{2,1,0:T(8,128)}, u32[]{:S(2)}) copy-start(f32[2,256,256]{2,1,0:T(8,128)} %u_ref.1) | copy-start | bytes 1572868
  153.2 6.2 %copy-start.1 = (f32[16,64,256]{2,1,0:T(8,128)}, f32[16,64,256]{2,1,0:T(8,128)S(1)}, u32[]{:S(2)}) copy-start(f32[16,64,256]{2,1,0:T(8,128)S(1)} %all-to-all-done.1) | copy-start | bytes 3145732
  153.2 29.7 %all-to-all-start = ((f32[16,64,256]{2,1,0:T(8,128)}), f32[16,64,256]{2,1,0:T(8,128)S(1)}, u32[]{:S(2)}, u32[]{:S(2)}) async-start(f32[16,64,256]{2,1,0:T(8,128)} %shard_map.93), calls=%async_computation | async-start | bytes 2097152 | tf_op jit(solution)/shard_map/all_to_all | solution.py:426
  182.9 1.0 copy-start.2

commit v4 on v3

--- a/solution.py
+++ b/solution.py
@@ -72,14 +72,6 @@
             out_specs=pl.BlockSpec(shape, lambda c, *_: (0, 0, 0)),
         ),
     )(odd, own, other, factors)
-
-
-def chip_at(place, chips):
-    return jnp.where(place < chips // 2, 2 * place, 2 * (chips - 1 - place) + 1)
-
-
-def place_of(chip, chips):
-    return jnp.where(chip % 2 == 0, chip // 2, chips - 1 - chip // 2)
 
 
 def leaf_block(listed, odd, m_ref, u_ref, out_ref, tops_ref, first, parts):
@@ -128,20 +120,22 @@
 
 def exchange_kernel(count, listed, odd, m_ref, y_ref, l_ref, u_ref, p_ref, work_ref, g_ref, r_ref, *rest):
     parts = rest[:8]
-    t_ref, ring_send, ring_recv, pass_send, pass_recv, a2a_send, a2a_recv, own_sem = rest[8:]
+    t_ref, ring_send, ring_recv, side_send, side_recv, pass_send, pass_recv, a2a_send, a2a_recv, own_sem = rest[8:]
     turn = pl.program_id(0)
     turns = t_ref.shape[0] // m_ref.shape[1]
     me = lax.axis_index("row")
     chips = count // 2
     share = t_ref.shape[0] // count
     core = me % 2
-    place = place_of(me // 2, chips)
-
-    def device(offset):
-        return chip_at((place + offset + chips) % chips, chips) * 2 + core
+    depth = chips // 2
+    lane = (me // 2) % 2
+    level = me // 4
+
+    def device(at, on):
+        return ((at + depth) % depth * 2 + on) * 2 + core
 
     partner = me + 1 - 2 * core
-    right, left = device(1), device(-1)
+    right, left, across = device(level + 1, lane), device(level - 1, lane), device(level, 1 - lane)
 
     def remote(source, target, send_sem, recv_sem, peer):
         return pltpu.make_async_remote_copy(
@@ -153,30 +147,46 @@
             device_id_type=pl.DeviceIdType.MESH,
         )
 
-    lengths = {(0, 0): chips // 2, (0, 1): chips - 1 - chips // 2}
-    lengths[1, 1], lengths[1, 0] = lengths[0, 0], lengths[0, 1]
-    longest = max(lengths.values())
+    ways = [(s, way) for s in range(STEPS) for way in range(2)]
+    slots = 2 * depth - 1
+
+    def arrives(way, t):
+        return level >= t + 1 if way == 0 else level + t + 1 <= depth - 1
+
+    def leaves(way, t):
+        return (level >= t) & (level < depth - 1) if way == 0 else (level + t < depth) & (level > 0)
+
+    def origin_of(way, t):
+        return level - t if way == 0 else level + t
+
+    def slot_of(way, t):
+        return 1 + t if way == 0 else depth + t
 
     def hop(s, way, t):
-        origin = device(-t if way == 0 else t)
-        source = p_ref.at[s] if t == 0 else g_ref.at[origin, s]
+        target = g_ref.at[device(origin_of(way, t), lane), s]
         return remote(
-            source,
-            g_ref.at[origin, s],
+            p_ref.at[s] if t == 0 else target,
+            target,
             ring_send.at[s, way, t],
             ring_recv.at[s, way, t],
             right if way == 0 else left,
         )
 
-    def hand(s, way, t):
+    def side(s, way, t):
         if t < 0:
-            return remote(
-                p_ref.at[s], g_ref.at[me, s], pass_send.at[s, 0], pass_recv.at[s, 0], partner
-            )
-        origin = device(-t - 1 if way == 0 else t + 1)
-        slot = 1 + (t if way == 0 else lengths[s, 0] + t)
-        piece = g_ref.at[origin, s]
-        return remote(piece, piece, pass_send.at[s, slot], pass_recv.at[s, slot], partner)
+            target, slot = g_ref.at[me, s], 0
+        else:
+            target, slot = g_ref.at[device(origin_of(way, t + 1), lane), s], slot_of(way, t)
+        source = p_ref.at[s] if t < 0 else target
+        return remote(source, target, side_send.at[s, slot], side_recv.at[s, slot], across)
+
+    def hand(s, way, t, turned):
+        on = 1 - lane if turned else lane
+        slot = 0 if t < 0 else slot_of(way, t)
+        target = g_ref.at[device(level if t < 0 else origin_of(way, t + 1), on), s]
+        source = p_ref.at[s] if t < 0 and not turned else target
+        slot += slots if turned else 0
+        return remote(source, target, pass_send.at[s, slot], pass_recv.at[s, slot], partner)
 
     def columns_of(peer):
         return t_ref.at[pl.ds(pl.multiple_of(peer * share, 8), share), :]
@@ -192,12 +202,48 @@
         return pltpu.make_async_copy(columns_of(me), r_ref.at[me], own_sem.at[STEPS])
 
     def advance(t):
-        for s, way in lengths:
-            if t < lengths[s, way]:
+        for s, way in ways:
+
+            @pl.when(arrives(way, t))
+            def _():
                 hop(s, way, t).wait_recv()
-                if t + 1 < lengths[s, way]:
-                    hop(s, way, t + 1).start()
-                hand(s, way, t).start()
+                if t + 1 < depth - 1:
+
+                    @pl.when(leaves(way, t + 1))
+                    def _():
+                        hop(s, way, t + 1).start()
+
+                side(s, way, t).start()
+                hand(s, way, t, False).start()
+
+    def relay(t):
+        for s, way in ways if t >= 0 else [(s, 0) for s in range(STEPS)]:
+
+            def move():
+                side(s, way, t).wait_recv()
+                hand(s, way, t, True).start()
+
+            if t < 0:
+                move()
+            else:
+                pl.when(arrives(way, t))(move)
+
+    def finish(t):
+        for s, way in ways if t >= 0 else [(s, 0) for s in range(STEPS)]:
+
+            def end():
+                side(s, way, t).wait_send()
+                hand(s, way, t, False).wait()
+                hand(s, way, t, True).wait()
+
+            if t < 0:
+                end()
+            else:
+                pl.when(arrives(way, t))(end)
+
+                @pl.when(leaves(way, t))
+                def _():
+                    hop(s, way, t).wait_send()
 
     @pl.when(turn == 0)
     def _():
@@ -210,11 +256,15 @@
                 device_id_type=pl.DeviceIdType.MESH,
             )
         pl.semaphore_wait(barrier, count - 1)
-        for s, way in lengths:
-            if lengths[s, way] > 0:
+        for s, way in ways:
+
+            @pl.when(leaves(way, 0))
+            def _():
                 hop(s, way, 0).start()
+
         for s in range(STEPS):
-            hand(s, 0, -1).start()
+            side(s, 0, -1).start()
+            hand(s, 0, -1, False).start()
             keep(s).start()
         yh, yl, yth, ytl, lth, ltl, uh, ul = parts
         for s in range(STEPS):
@@ -226,29 +276,27 @@
     first = pl.multiple_of(turn * m_ref.shape[1], m_ref.shape[1])
     leaf_block(listed, odd, m_ref, u_ref, work_ref, t_ref, first, parts)
 
-    early = min(turns - 1, longest)
+    early = min(turns - 1, depth - 1)
     for t in range(early):
 
         @pl.when(turn == t)
         def _():
             advance(t)
+            relay(t - 1)
 
     @pl.when(turn == turns - 1)
     def _():
+        for t in range(early, depth - 1):
+            advance(t)
+            relay(t - 1)
         todo = [(j + count // 2 - 1) % (count - 1) + 1 for j in range(count - 1)]
-        rounds = max(longest - early, 1)
-        size = -(-len(todo) // rounds)
         keep_columns().start()
-        for t in range(rounds):
-            for j in todo[t * size : (t + 1) * size]:
-                scatter(j).start()
-            advance(early + t)
-        for s, way in lengths:
-            for t in range(lengths[s, way]):
-                hop(s, way, t).wait_send()
-                hand(s, way, t).wait()
+        for j in todo:
+            scatter(j).start()
+        relay(depth - 2)
+        for t in range(-1, depth - 1):
+            finish(t)
         for s in range(STEPS):
-            hand(s, 0, -1).wait()
             keep(s).wait()
         keep_columns().wait()
         for j in todo:
@@ -293,10 +341,12 @@
                 *[pltpu.VMEM((steps, panel, leaf_rows), half_type)] * 2,
                 *[pltpu.VMEM((steps, panel, panel), half_type)] * 4,
                 pltpu.VMEM((columns, steps * panel), jnp.float32),
-                dma((steps, 2, chips)),
-                dma((steps, 2, chips)),
-                dma((steps, chips)),
-                dma((steps, chips)),
+                dma((steps, 2, chips // 2)),
+                dma((steps, 2, chips // 2)),
+                dma((steps, chips - 1)),
+                dma((steps, chips - 1)),
+                dma((steps, 2 * chips - 2)),
+                dma((steps, 2 * chips - 2)),
                 dma((count - 1,)),
                 dma((count - 1,)),
                 dma((steps + 1,)),
@@ -363,19 +413,28 @@
     )(upper, lower, spread, reflectors)
 
 
+def place_rows(flag, back_ref, u_ref, rows_ref, out_ref):
+    @pl.when(flag == 0)
+    def _():
+        out_ref[...] = back_ref[...].T
+
+    @pl.when(flag == 1)
+    def _():
+        out_ref[...] = rows_ref[...] - product3(split(u_ref[...]), split(back_ref[...]), NT)
+
+
 def place_kernel(odd, back_ref, u_ref, work_ref, out_ref):
-    @pl.when(odd[0] == 0)
-    def _():
-        out_ref[...] = back_ref[...].T
-
-    @pl.when(odd[0] == 1)
-    def _():
-        out_ref[...] = work_ref[...] - product3(split(u_ref[...]), split(back_ref[...]), NT)
+    panel = u_ref.shape[0]
+    rows = out_ref.shape[0]
+    place_rows(odd[0], back_ref, u_ref, work_ref.at[:panel], out_ref.at[:panel])
+    if rows > panel:
+        out_ref[panel:, :] = work_ref[panel:, :]
 
 
 def place(step, back, vectors, work, odd):
     columns, panel = back.shape
     width = COLS_PER_LEAF
+    rows = work.shape[0] if step == 0 else panel
     return pl.pallas_call(
         place_kernel,
         out_shape=jax.ShapeDtypeStruct(work.shape, jnp.float32),
@@ -385,11 +444,11 @@
             in_specs=[
                 pl.BlockSpec((width, panel), lambda c, *_: (c, 0)),
                 pl.BlockSpec((panel, panel), lambda c, *_: (0, 0)),
-                pl.BlockSpec((panel, width), lambda c, *_: (step, c)),
+                pl.BlockSpec((rows, width), lambda c, *_: (step, c)),
             ],
-            out_specs=pl.BlockSpec((panel, width), lambda c, *_: (step, c)),
+            out_specs=pl.BlockSpec((rows, width), lambda c, *_: (step, c)),
         ),
-        input_output_aliases={3: 0},
+        input_output_aliases={} if step == 0 else {3: 0},
     )(odd, back, vectors, work)
 
 

time: 195 us -> 195 us (level)
  local copies, waits for them, and re-layouts: 11.1 us -> 6.27 us
  Pallas kernels: 136 us -> 140 us
  starting transfers between devices: 14.2 us -> 17.2 us
    unnamed x11 -> x10, local copies, waits for them, and re-layouts: 6.47 us -> 1.7 us
    all_to_all x2, starting transfers between devices: 13.6 us -> 16.5 us  [shards(): back = lax.all_to_all(done, 'row', 0, 0).reshape(columns, panel)]
    pallas_call x1, Pallas kernels: 93.4 us -> 95.8 us  [exchange(): pl.pallas_call(functools.partial(exchange_kernel, count), out_shape=(jax....]
  transfers between devices with their start and end apart: 3 -> 3, of which waited for: 2 -> 2; matrix products, arithmetic and copies ran while one was open for 3% -> 3% of each run, Pallas kernels for 10% -> 11%
where the time goes in v4:
time: 195 us; the launch traced here: 194 us
  Pallas kernels  140 us (72%)
  waiting for transfers between devices  26.9 us (14%)
  starting transfers between devices  17.2 us (9%)
  local copies, waits for them, and re-layouts  6.27 us (3%)
  other arithmetic  3.74 us (2%)
    pallas_call x1, Pallas kernels, exchange(): pl.pallas_call(functools.partial(exchange_kernel, count), out_shape=(jax....  95.8 us
    pallas_call x2, Pallas kernels, tree(): pl.pallas_call(tree_kernel, out_shape=jax.ShapeDtypeStruct(block, jnp.flo...  30 us
    all_to_all x2, waiting for transfers between devices, shards(): back = lax.all_to_all(done, 'row', 0, 0).reshape(columns, panel)  26.9 us
    all_to_all x2, starting transfers between devices, shards(): back = lax.all_to_all(done, 'row', 0, 0).reshape(columns, panel)  16.5 us
    pallas_call x2, Pallas kernels, place(): pl.pallas_call(place_kernel, out_shape=jax.ShapeDtypeStruct(work.shape, j...  11.3 us
  transfers between devices with their start and end apart: 3, of which 2 were waited for; matrix products, arithmetic and copies ran while one was open for 3% of the time, Pallas kernels for 11%

profile of v4, /device:TPU:11, one launch (start us, length us, event | category | flops | bytes accessed | tf_op | source)
XLA Modules:
  0.0 194.1 jit_solution(7640469530850275814)
XLA Ops:
  0.0 1.8 constant_dynamic-slice_fusion
  1.8 0.7 collective-permute-start
  2.4 1.2 and_select_fusion.4.odd
  3.6 1.3 fusion.5
  5.0 2.6 %and_select_fusion = (s32[15]{0:T(128)}, s32[15]{0:T(128)}, s32[15]{0:T(128)}, s32[15]{0:T(128)}) fusion(s32[15]{0:T(128)} %constant.65.clone, s32[]{:T(128)} %bitcast.3, s32[]{:T(128)} %bitcast, s32[15]{0:T(128)} %constant.64.clone), kind=kLoop, calls=%fused_computation.12 | loop fusion | flops 720 | bytes 368 | tf_op jit(solution)/shard_map/jit(remainder)/select_n | solution.py:483
  7.5 0.0 collective-permute-done.other_ref
  7.5 0.0 copy-start.3
  7.5 0.7 copy-done.3
  8.2 2.9 %shard_map.91.p_ref = f32[2,264,256]{2,1,0:T(8,128)} custom-call(s32[2]{0:T(128)} %and_select_fusion.4.odd, f32[2,128,256]{2,1,0:T(8,128)} %get-tuple-element.14.own_ref, f32[2,128,256]{2,1,0:T(8,128)} %copy-done.3, f32[2,256,256]{2,1,0:T(8,128)} %f_ref.1), custom_call_target="tpu_custom_call" | custom-call | tf_op jit(solution)/shard_map/pallas_call | solution.py:61
  11.1 95.8 %shard_map.92 = (f32[1024,1024]{1,0:T(8,128)}, f32[16,2,264,256]{3,2,1,0:T(8,128)}, f32[16,64,512]{2,1,0:T(8,128)}) custom-call(s32[2,5]{1,0:T(2,128)} %listed.1, s32[2]{0:T(128)} %and_select_fusion.4.odd, f32[1024,1024]{1,0:T(8,128)} %m_ref.1, f32[2,640,256]{2,1,0:T(8,128)} %y_ref.1, f32[2,256,256]{2,1,0:T(8,128)} %l_ref.1, f32[2,256,256]{2,1,0:T(8,128)} %u_ref.1, ...), custom_call_target="tpu_custom_call" | custom-call | tf_op jit(solution)/shard_map/pallas_call | solution.py:317
  106.9 14.9 %shard_map.94 = f32[16,64,256]{2,1,0:T(8,128)} custom-call(s32[15]{0:T(128)} %get-tuple-element.24.upper, s32[15]{0:T(128)} %get-tuple-element.15.lower, f32[16,64,512]{2,1,0:T(8,128)} %get-tuple-element.8.x_ref, f32[16,2,264,256]{3,2,1,0:T(8,128)} %get-tuple-element.9.g_ref), custom_call_target="tpu_custom_call" | custom-call | tf_op jit(solution)/shard_map/pallas_call | solution.py:399
  121.8 11.8 %all-to-all-start.1 = ((f32[16,64,256]{2,1,0:T(8,128)}), f32[16,64,256]{2,1,0:T(8,128)S(1)}, u32[]{:S(2)}, u32[]{:S(2)}) async-start(f32[16,64,256]{2,1,0:T(8,128)} %shard_map.94), calls=%async_computation.1 | async-start | bytes 2097152 | tf_op jit(solution)/shard_map/all_to_all | solution.py:485
  133.6 0.0 copy-start.4
  133.6 0.0 copy-start
  133.6 15.1 %shard_map.93 = f32[16,64,256]{2,1,0:T(8,128)} custom-call(s32[15]{0:T(128)} %get-tuple-element.23.upper, s32[15]{0:T(128)} %get-tuple-element.16.lower, f32[16,64,512]{2,1,0:T(8,128)} %get-tuple-element.8.x_ref, f32[16,2,264,256]{3,2,1,0:T(8,128)} %get-tuple-element.9.g_ref), custom_call_target="tpu_custom_call" | custom-call | tf_op jit(solution)/shard_map/pallas_call | solution.py:399
  148.8 9.8 %all-to-all-done.1 = f32[16,64,256]{2,1,0:T(8,128)S(1)} async-done(((f32[16,64,256]{2,1,0:T(8,128)}), f32[16,64,256]{2,1,0:T(8,128)S(1)}, u32[]{:S(2)}, u32[]{:S(2)}) %all-to-all-start.1) | async-done | bytes 1048608 | tf_op jit(solution)/shard_map/all_to_all | solution.py:485
  158.6 0.0 copy-start.1
  158.6 4.7 %all-to-all-start = ((f32[16,64,256]{2,1,0:T(8,128)}), f32[16,64,256]{2,1,0:T(8,128)S(1)}, u32[]{:S(2)}, u32[]{:S(2)}) async-start(f32[16,64,256]{2,1,0:T(8,128)} %shard_map.93), calls=%async_computation | async-start | bytes 2097152 | tf_op jit(solution)/shard_map/all_to_all | solution.py:485
  163.3 0.0 copy-done.4
  163.3 0.6 fusion.6
  163.9 0.0 copy-done
  163.9 0.8 slice_bitcast_fusion
  164.8 0.0 copy-done.1
  164.8 6.4 %shard_map.95.work_ref = f32[1024,1024]{1,0:T(8,128)} custom-call(s32[1]{0:T(128)} %get-tuple-element.21.odd, f32[1024,256]{1,0:T(8,128)} %bitcast.8, f32[256,256]{1,0:T(8,128)} %get-tuple-element.11.u_ref, f32[1024,1024]{1,0:T(8,128)} %get-tuple-element.10.work_ref), custom_call_target="tpu_custom_call" | custom-call | tf_op jit(solution)/shard_map/pallas_call | solution.py:438
  171.2 17.1 %all-to-all-done = f32[16,64,256]{2,1,0:T(8,128)S(1)} async-done(((f32[16,64,256]{2,1,0:T(8,128)}), f32[16,64,256]{2,1,0:T(8,128)S(1)}, u32[]{:S(2)}, u32[]{:S(2)}) %all-to-all-start) | async-done | bytes 1048608 | tf_op jit(solution)/shard_map/all_to_all | solution.py:485
  188.2 0.0 copy-start.2
  188.2 1.0 copy-done.2
  189.2 4.9 %shard_map.96 = f32[1024,1024]{1,0:T(8,128)} custom-call(s32[1]{0:T(128)} %get-tuple-element.22.odd, f32[1024,256]{1,0:T(8,128)} %bitcast.9, f32[256,256]{1,0:T(8,128)} %get-tuple-element.12.u_ref, f32[1024,1024]{1,0:T(8,128)} %shard_map.95.work_ref), custom_call_target="tpu_custom_call", output_to_operand_aliasing={{}: (3, {})} | custom-call | tf_op jit(solution)/shard_map/pallas_call | solution.py:438
Async XLA Ops:
  1.8 5.8 %collective-permute-start = (f32[2,128,256]{2,1,0:T(8,128)S(1)}, f32[2,128,256]{2,1,0:T(8,128)S(1)}, u32[]{:S(2)}, u32[]{:S(2)}) collective-permute-start(f32[2,128,256]{2,1,0:T(8,128)S(1)} %get-tuple-element.13), channel_id=1, source_target_pairs={{0,1},{1,0},{2,3},{3,2},{4,5},{5,4},{6,7},{7,6},{8,9},{9,8},{10,11... | collective-permute-start | bytes 786440 | tf_op jit(solution)/shard_map/ppermute | solution.py:476
  7.5 0.7 copy-start.3
  121.8 36.8 %all-to-all-start.1 = ((f32[16,64,256]{2,1,0:T(8,128)}), f32[16,64,256]{2,1,0:T(8,128)S(1)}, u32[]{:S(2)}, u32[]{:S(2)}) async-start(f32[16,64,256]{2,1,0:T(8,128)} %shard_map.94), calls=%async_computation.1 | async-start | bytes 2097152 | tf_op jit(solution)/shard_map/all_to_all | solution.py:485
  133.6 29.7 %copy-start.4 = (s32[2]{0:T(128)S(1)}, s32[2]{0:T(128)}, u32[]{:S(2)}) copy-start(s32[2]{0:T(128)} %and_select_fusion.4.odd) | copy-start | bytes 28
  133.6 30.3 %copy-start = (f32[2,256,256]{2,1,0:T(8,128)S(1)}, f32[2,256,256]{2,1,0:T(8,128)}, u32[]{:S(2)}) copy-start(f32[2,256,256]{2,1,0:T(8,128)} %u_ref.1) | copy-start | bytes 1572868
  158.6 6.2 %copy-start.1 = (f32[16,64,256]{2,1,0:T(8,128)}, f32[16,64,256]{2,1,0:T(8,128)S(1)}, u32[]{:S(2)}) copy-start(f32[16,64,256]{2,1,0:T(8,128)S(1)} %all-to-all-done.1) | copy-start | bytes 3145732
  158.6 29.6 %all-to-all-start = ((f32[16,64,256]{2,1,0:T(8,128)}), f32[16,64,256]{2,1,0:T(8,128)S(1)}, u32[]{:S(2)}, u32[]{:S(2)}) async-start(f32[16,64,256]{2,1,0:T(8,128)} %shard_map.93), calls=%async_computation | async-start | bytes 2097152 | tf_op jit(solution)/shard_map/all_to_all | solution.py:485
  188.2 1.0 copy-start.2

commit v5 on v3

--- a/solution.py
+++ b/solution.py
@@ -363,19 +363,28 @@
     )(upper, lower, spread, reflectors)
 
 
+def place_rows(flag, back_ref, u_ref, rows_ref, out_ref):
+    @pl.when(flag == 0)
+    def _():
+        out_ref[...] = back_ref[...].T
+
+    @pl.when(flag == 1)
+    def _():
+        out_ref[...] = rows_ref[...] - product3(split(u_ref[...]), split(back_ref[...]), NT)
+
+
 def place_kernel(odd, back_ref, u_ref, work_ref, out_ref):
-    @pl.when(odd[0] == 0)
-    def _():
-        out_ref[...] = back_ref[...].T
-
-    @pl.when(odd[0] == 1)
-    def _():
-        out_ref[...] = work_ref[...] - product3(split(u_ref[...]), split(back_ref[...]), NT)
+    panel = u_ref.shape[0]
+    rows = out_ref.shape[0]
+    place_rows(odd[0], back_ref, u_ref, work_ref.at[:panel], out_ref.at[:panel])
+    if rows > panel:
+        out_ref[panel:, :] = work_ref[panel:, :]
 
 
 def place(step, back, vectors, work, odd):
     columns, panel = back.shape
     width = COLS_PER_LEAF
+    rows = work.shape[0] if step == 0 else panel
     return pl.pallas_call(
         place_kernel,
         out_shape=jax.ShapeDtypeStruct(work.shape, jnp.float32),
@@ -385,11 +394,11 @@
             in_specs=[
                 pl.BlockSpec((width, panel), lambda c, *_: (c, 0)),
                 pl.BlockSpec((panel, panel), lambda c, *_: (0, 0)),
-                pl.BlockSpec((panel, width), lambda c, *_: (step, c)),
-            ],
-            out_specs=pl.BlockSpec((panel, width), lambda c, *_: (step, c)),
-        ),
-        input_output_aliases={3: 0},
+                pl.BlockSpec((rows, width), lambda c, *_: (step, c)),
+            ],
+            out_specs=pl.BlockSpec((rows, width), lambda c, *_: (step, c)),
+        ),
+        input_output_aliases={} if step == 0 else {3: 0},
     )(odd, back, vectors, work)
 
 

time: 195 us -> 190 us (0.974)
  local copies, waits for them, and re-layouts: 11.1 us -> 6.27 us
  Pallas kernels: 136 us -> 138 us
    unnamed x11 -> x10, local copies, waits for them, and re-layouts: 6.47 us -> 1.7 us
  transfers between devices with their start and end apart: 3 -> 3, of which waited for: 2 -> 2; matrix products, arithmetic and copies ran while one was open for 3% -> 3% of each run, Pallas kernels for 10% -> 11%
where the time goes in v5:
time: 190 us; the launch traced here: 189 us
  Pallas kernels  138 us (73%)
  waiting for transfers between devices  26.9 us (14%)
  starting transfers between devices  14.2 us (7%)
  local copies, waits for them, and re-layouts  6.27 us (3%)
  other arithmetic  3.74 us (2%)
    pallas_call x1, Pallas kernels, exchange(): pl.pallas_call(functools.partial(exchange_kernel, count), out_shape=(jax....  93.4 us
    pallas_call x2, Pallas kernels, tree(): pl.pallas_call(tree_kernel, out_shape=jax.ShapeDtypeStruct(block, jnp.flo...  30 us
    all_to_all x2, waiting for transfers between devices, shards(): back = lax.all_to_all(done, 'row', 0, 0).reshape(columns, panel)  26.9 us
    all_to_all x2, starting transfers between devices, shards(): back = lax.all_to_all(done, 'row', 0, 0).reshape(columns, panel)  13.6 us
    pallas_call x2, Pallas kernels, place(): pl.pallas_call(place_kernel, out_shape=jax.ShapeDtypeStruct(work.shape, j...  11.3 us
  transfers between devices with their start and end apart: 3, of which 2 were waited for; matrix products, arithmetic and copies ran while one was open for 3% of the time, Pallas kernels for 11%

profile of v5, /device:TPU:11, one launch (start us, length us, event | category | flops | bytes accessed | tf_op | source)
XLA Modules:
  0.0 188.7 jit_solution(5456509904131514267)
XLA Ops:
  0.0 1.8 constant_dynamic-slice_fusion
  1.8 0.7 collective-permute-start
  2.4 1.2 and_select_fusion.4.odd
  3.6 1.3 fusion.5
  5.0 2.6 %and_select_fusion = (s32[15]{0:T(128)}, s32[15]{0:T(128)}, s32[15]{0:T(128)}, s32[15]{0:T(128)}) fusion(s32[15]{0:T(128)} %constant.65.clone, s32[]{:T(128)} %bitcast.3, s32[]{:T(128)} %bitcast, s32[15]{0:T(128)} %constant.64.clone), kind=kLoop, calls=%fused_computation.12 | loop fusion | flops 720 | bytes 368 | tf_op jit(solution)/shard_map/jit(remainder)/select_n | solution.py:433
  7.5 0.0 collective-permute-done.other_ref
  7.5 0.0 copy-start.3
  7.5 0.7 copy-done.3
  8.2 2.9 %shard_map.91.p_ref = f32[2,264,256]{2,1,0:T(8,128)} custom-call(s32[2]{0:T(128)} %and_select_fusion.4.odd, f32[2,128,256]{2,1,0:T(8,128)} %get-tuple-element.14.own_ref, f32[2,128,256]{2,1,0:T(8,128)} %copy-done.3, f32[2,256,256]{2,1,0:T(8,128)} %f_ref.1), custom_call_target="tpu_custom_call" | custom-call | tf_op jit(solution)/shard_map/pallas_call | solution.py:61
  11.1 93.4 %shard_map.92 = (f32[1024,1024]{1,0:T(8,128)}, f32[16,2,264,256]{3,2,1,0:T(8,128)}, f32[16,64,512]{2,1,0:T(8,128)}) custom-call(s32[2,5]{1,0:T(2,128)} %listed.1, s32[2]{0:T(128)} %and_select_fusion.4.odd, f32[1024,1024]{1,0:T(8,128)} %m_ref.1, f32[2,640,256]{2,1,0:T(8,128)} %y_ref.1, f32[2,256,256]{2,1,0:T(8,128)} %l_ref.1, f32[2,256,256]{2,1,0:T(8,128)} %u_ref.1, ...), custom_call_target="tpu_custom_call" | custom-call | tf_op jit(solution)/shard_map/pallas_call | solution.py:269
  104.5 14.9 %shard_map.94 = f32[16,64,256]{2,1,0:T(8,128)} custom-call(s32[15]{0:T(128)} %get-tuple-element.24.upper, s32[15]{0:T(128)} %get-tuple-element.15.lower, f32[16,64,512]{2,1,0:T(8,128)} %get-tuple-element.8.x_ref, f32[16,2,264,256]{3,2,1,0:T(8,128)} %get-tuple-element.9.g_ref), custom_call_target="tpu_custom_call" | custom-call | tf_op jit(solution)/shard_map/pallas_call | solution.py:349
  119.4 8.8 %all-to-all-start.1 = ((f32[16,64,256]{2,1,0:T(8,128)}), f32[16,64,256]{2,1,0:T(8,128)S(1)}, u32[]{:S(2)}, u32[]{:S(2)}) async-start(f32[16,64,256]{2,1,0:T(8,128)} %shard_map.94), calls=%async_computation.1 | async-start | bytes 2097152 | tf_op jit(solution)/shard_map/all_to_all | solution.py:435
  128.2 0.0 copy-start.4
  128.2 0.0 copy-start
  128.2 15.1 %shard_map.93 = f32[16,64,256]{2,1,0:T(8,128)} custom-call(s32[15]{0:T(128)} %get-tuple-element.23.upper, s32[15]{0:T(128)} %get-tuple-element.16.lower, f32[16,64,512]{2,1,0:T(8,128)} %get-tuple-element.8.x_ref, f32[16,2,264,256]{3,2,1,0:T(8,128)} %get-tuple-element.9.g_ref), custom_call_target="tpu_custom_call" | custom-call | tf_op jit(solution)/shard_map/pallas_call | solution.py:349
  143.3 9.8 %all-to-all-done.1 = f32[16,64,256]{2,1,0:T(8,128)S(1)} async-done(((f32[16,64,256]{2,1,0:T(8,128)}), f32[16,64,256]{2,1,0:T(8,128)S(1)}, u32[]{:S(2)}, u32[]{:S(2)}) %all-to-all-start.1) | async-done | bytes 1048608 | tf_op jit(solution)/shard_map/all_to_all | solution.py:435
  153.1 0.0 copy-start.1
  153.1 4.8 %all-to-all-start = ((f32[16,64,256]{2,1,0:T(8,128)}), f32[16,64,256]{2,1,0:T(8,128)S(1)}, u32[]{:S(2)}, u32[]{:S(2)}) async-start(f32[16,64,256]{2,1,0:T(8,128)} %shard_map.93), calls=%async_computation | async-start | bytes 2097152 | tf_op jit(solution)/shard_map/all_to_all | solution.py:435
  157.9 0.0 copy-done.4
  157.9 0.6 fusion.6
  158.5 0.0 copy-done
  158.5 0.8 slice_bitcast_fusion
  159.4 0.0 copy-done.1
  159.4 6.4 %shard_map.95.work_ref = f32[1024,1024]{1,0:T(8,128)} custom-call(s32[1]{0:T(128)} %get-tuple-element.21.odd, f32[1024,256]{1,0:T(8,128)} %bitcast.8, f32[256,256]{1,0:T(8,128)} %get-tuple-element.11.u_ref, f32[1024,1024]{1,0:T(8,128)} %get-tuple-element.10.work_ref), custom_call_target="tpu_custom_call" | custom-call | tf_op jit(solution)/shard_map/pallas_call | solution.py:388
  165.7 17.1 %all-to-all-done = f32[16,64,256]{2,1,0:T(8,128)S(1)} async-done(((f32[16,64,256]{2,1,0:T(8,128)}), f32[16,64,256]{2,1,0:T(8,128)S(1)}, u32[]{:S(2)}, u32[]{:S(2)}) %all-to-all-start) | async-done | bytes 1048608 | tf_op jit(solution)/shard_map/all_to_all | solution.py:435
  182.8 0.0 copy-start.2
  182.8 1.0 copy-done.2
  183.8 4.9 %shard_map.96 = f32[1024,1024]{1,0:T(8,128)} custom-call(s32[1]{0:T(128)} %get-tuple-element.22.odd, f32[1024,256]{1,0:T(8,128)} %bitcast.9, f32[256,256]{1,0:T(8,128)} %get-tuple-element.12.u_ref, f32[1024,1024]{1,0:T(8,128)} %shard_map.95.work_ref), custom_call_target="tpu_custom_call", output_to_operand_aliasing={{}: (3, {})} | custom-call | tf_op jit(solution)/shard_map/pallas_call | solution.py:388
Async XLA Ops:
  1.8 5.8 %collective-permute-start = (f32[2,128,256]{2,1,0:T(8,128)S(1)}, f32[2,128,256]{2,1,0:T(8,128)S(1)}, u32[]{:S(2)}, u32[]{:S(2)}) collective-permute-start(f32[2,128,256]{2,1,0:T(8,128)S(1)} %get-tuple-element.13), channel_id=1, source_target_pairs={{0,1},{1,0},{2,3},{3,2},{4,5},{5,4},{6,7},{7,6},{8,9},{9,8},{10,11... | collective-permute-start | bytes 786440 | tf_op jit(solution)/shard_map/ppermute | solution.py:426
  7.5 0.7 copy-start.3
  119.4 33.7 %all-to-all-start.1 = ((f32[16,64,256]{2,1,0:T(8,128)}), f32[16,64,256]{2,1,0:T(8,128)S(1)}, u32[]{:S(2)}, u32[]{:S(2)}) async-start(f32[16,64,256]{2,1,0:T(8,128)} %shard_map.94), calls=%async_computation.1 | async-start | bytes 2097152 | tf_op jit(solution)/shard_map/all_to_all | solution.py:435
  128.2 29.7 %copy-start.4 = (s32[2]{0:T(128)S(1)}, s32[2]{0:T(128)}, u32[]{:S(2)}) copy-start(s32[2]{0:T(128)} %and_select_fusion.4.odd) | copy-start | bytes 28
  128.2 30.3 %copy-start = (f32[2,256,256]{2,1,0:T(8,128)S(1)}, f32[2,256,256]{2,1,0:T(8,128)}, u32[]{:S(2)}) copy-start(f32[2,256,256]{2,1,0:T(8,128)} %u_ref.1) | copy-start | bytes 1572868
  153.1 6.3 %copy-start.1 = (f32[16,64,256]{2,1,0:T(8,128)}, f32[16,64,256]{2,1,0:T(8,128)S(1)}, u32[]{:S(2)}) copy-start(f32[16,64,256]{2,1,0:T(8,128)S(1)} %all-to-all-done.1) | copy-start | bytes 3145732
  153.1 29.7 %all-to-all-start = ((f32[16,64,256]{2,1,0:T(8,128)}), f32[16,64,256]{2,1,0:T(8,128)S(1)}, u32[]{:S(2)}, u32[]{:S(2)}) async-start(f32[16,64,256]{2,1,0:T(8,128)} %shard_map.93), calls=%async_computation | async-start | bytes 2097152 | tf_op jit(solution)/shard_map/all_to_all | solution.py:435
  182.8 1.0 copy-start.2
